TPU v7x, 32 devices: a whole 2x2x4 slice. The times are simulated.
32 devices in a mesh: leaf: 16 (over z, y, x), front: 2 (over core).
Axes of the slice: x: 2, y: 2, z: 4, core: 2. Of those that a mesh axis runs over, the one named last changes fastest.
Arguments:
- child_fronts: float32 [48, 2, 512, 1024], P('leaf', None, 'front'), may hold values from 0 to 16, as said below
- child_live: int32 [16], P('leaf'), may hold values from 1 to 3, as said below
- row_map: int32 [48, 4], P('leaf'), may hold values from 0 to 7, as said below
- parent_fronts: float32 [16, 2, 256, 1024], P('leaf', None, 'front'), may hold values from 0 to 16, as said below
Outputs:
- child_panels: float32 [48, 2, 512, 512], P('leaf', None, 'front')
- parent_panels: float32 [16, 2, 256, 512], P('leaf', None, 'front')
- parent_updates: float32 [16, 256, 512], P('leaf', 'front')
Inputs may be any that keep to these rules, and one draw needn't show every extreme that they name: `child_fronts`: each front and each separator front is symmetric, and it and every separator front after the extend-add are positive definite. `parent_fronts`: symmetric as the child fronts. `child_live`: the two subtrees of leaf indices 2 * k and 2 * k + 1 hold at most 4 live fronts together; in every draw some subtree holds 3. `row_map`: each row names 4 different blocks of the separator, in increasing order.
All inputs are finite; a program needn't handle non-finite values.
Results may differ from a plain program's by a relative error of at most 0.000053.
Values sent between devices are 32-bit elements; how exact they have to be, the bound alone decides.
A program may use at most 128 MiB of HBM per device.

v0:
```python
import functools

import jax
import jax.numpy as jnp
from jax import lax
from jax.experimental import pallas as pl
from jax.experimental.pallas import tpu as pltpu
from jax.sharding import PartitionSpec as P

HIGHEST = lax.Precision.HIGHEST
LANES = 128
SUB = 8
GROUP = 4
VMEM_LIMIT = 60 * 1024 * 1024


def dot_nt(a, b):
    return lax.dot_general(
        a, b, (((1,), (1,)), ((), ())), precision=HIGHEST, preferred_element_type=jnp.float32
    )


def spread_lane(x, lane):
    return jnp.broadcast_to(x[:, lane : lane + 1], (SUB, LANES))


def spread_row(x, row):
    return jnp.broadcast_to(x[row : row + 1, :], (SUB, LANES))


def eliminate_group(tiles, start, lane_ids, row_ids):
    tile, first = divmod(start, SUB)
    size = GROUP
    rows = [spread_row(tiles[tile], first + k) for k in range(size)]
    entry = {}
    for k in range(size):
        for l in range(k + 1):
            entry[k, l] = spread_lane(rows[k], start + l)
    ratio = {}
    inverse = []
    for k in range(size):
        inverse.append(1.0 / entry[k, k])
        for m in range(k + 1, size):
            ratio[m, k] = entry[m, k] * inverse[k]
        for m in range(k + 1, size):
            for l in range(k + 1, m + 1):
                entry[m, l] = entry[m, l] - ratio[m, k] * entry[l, k]
    inside = (lane_ids >= start) & (lane_ids < start + size)
    for k in range(size):
        unit = jnp.where(lane_ids == start + k, 1.0, 0.0)
        rows[k] = jnp.where(inside, unit, rows[k])
    for k in range(size):
        for l in range(k):
            rows[k] = rows[k] - ratio[k, l] * rows[l]
    scaled = [rows[k] * inverse[k] for k in range(size)]
    result = list(tiles)
    for t in range(tile, len(tiles)):
        old = tiles[t]
        if t == tile and first + size == SUB:
            new = old
        else:
            factors = []
            for k in range(size):
                value = spread_lane(old, start + k)
                for l in range(k):
                    value = value - factors[l] * ratio[k, l]
                factors.append(value)
            new = jnp.where(inside, 0.0, old)
            total = factors[0] * scaled[0]
            for k in range(1, size):
                total = total + factors[k] * scaled[k]
            new = new - total
        if t == tile:
            new = jnp.where(row_ids < first, old, new)
            for k in range(size):
                root = lax.rsqrt(entry[k, k])
                new = jnp.where(row_ids == first + k, rows[k] * root, new)
        result[t] = new
    return result


def factor_inverses(blocks):
    lane_ids = lax.broadcasted_iota(jnp.int32, (SUB, LANES), 1)
    row_ids = lax.broadcasted_iota(jnp.int32, (SUB, LANES), 0)
    count = LANES // SUB
    tiles = [[b[t * SUB : (t + 1) * SUB, :] for t in range(count)] for b in blocks]
    for start in range(0, LANES, GROUP):
        tiles = [eliminate_group(t, start, lane_ids, row_ids) for t in tiles]
    rows = lax.broadcasted_iota(jnp.int32, (LANES, LANES), 0)
    columns = lax.broadcasted_iota(jnp.int32, (LANES, LANES), 1)
    return [jnp.where(columns <= rows, jnp.concatenate(t, axis=0), 0.0) for t in tiles]


def factor_panels(work, pivots):
    fronts, rows, _ = work.shape
    steps = pivots // LANES
    triangle = lax.broadcasted_iota(jnp.int32, (LANES, LANES), 1) <= lax.broadcasted_iota(
        jnp.int32, (LANES, LANES), 0
    )

    @pl.loop(0, steps)
    def _(step):
        here = pl.multiple_of(step * LANES, LANES)
        span = pl.ds(here, LANES)
        inverses = factor_inverses([work[f, span, span] for f in range(fronts)])
        for f in range(fronts):
            work[f, span, span] = jnp.where(
                triangle, dot_nt(work[f, span, span], inverses[f]), 0.0
            )

        @pl.loop(step + 1, rows // LANES)
        def _(below):
            low = pl.ds(pl.multiple_of(below * LANES, LANES), LANES)
            for f in range(fronts):
                work[f, low, span] = dot_nt(work[f, low, span], inverses[f])

        @pl.loop(step + 1, steps)
        def _(column):
            side = pl.ds(pl.multiple_of(column * LANES, LANES), LANES)
            others = [work[f, side, span] for f in range(fronts)]

            @pl.loop(column, rows // LANES)
            def _(below):
                low = pl.ds(pl.multiple_of(below * LANES, LANES), LANES)
                for f in range(fronts):
                    work[f, low, side] = work[f, low, side] - dot_nt(
                        work[f, low, span], others[f]
                    )


def clear_upper(work, pivots):
    for step in range(pivots // LANES):
        top = step * LANES
        if top + LANES < pivots:
            for f in range(work.shape[0]):
                work[f, top : top + LANES, top + LANES : pivots] = jnp.zeros(
                    (LANES, pivots - top - LANES), jnp.float32
                )


def child_kernel(place, own, other, out, work):
    core, live = place[0], place[1]
    slots, _, half, pivots = own.shape
    mine = pl.ds(pl.multiple_of(core * half, half), half)
    yours = pl.ds(pl.multiple_of((1 - core) * half, half), half)
    for s in range(slots):
        work[s, mine, :] = own[s, 0]
        work[s, yours, :] = other[s]
        work[s, 2 * half :, :] = own[s, 1]
    factor_panels(work, pivots)
    clear_upper(work, pivots)
    for s in range(slots):
        out[s, 0] = jnp.where(s < live, work[s, mine, :], 0.0)
        out[s, 1] = jnp.where(s < live, work[s, 2 * half :, :], 0.0)


def add_kernel(
    place, maps, own22, other22, own21, other21, parent, pivot_out, keep_out, send_out, whole
):
    core, live, half = place[0], place[1], place[2]
    slots, rows, width = own22.shape
    block = LANES
    per_core = rows // block
    blocks = width // block
    mine = pl.ds(pl.multiple_of(core * rows, rows), rows)
    yours = pl.ds(pl.multiple_of((1 - core) * rows, rows), rows)
    for s in range(slots):
        whole[s, mine, :] = own21[s]
        whole[s, yours, :] = other21[s]
    pivot_out[...] = jnp.zeros_like(pivot_out)
    keep_out[...] = parent[1]
    send_out[...] = jnp.zeros_like(send_out)
    pivot_out[half] = parent[0, :, : pivot_out.shape[2]]
    pivot_blocks = pivot_out.shape[2] // block

    @pl.loop(0, slots)
    def _(s):
        @pl.loop(0, blocks)
        def _(a):
            target = maps[s, a]

            @pl.when((s < live) & (target % 2 == core))
            def _():
                span = pl.ds(pl.multiple_of(a * block, block), block)
                low = pl.ds(pl.multiple_of((a % per_core) * block, block), block)
                is_mine = a // per_core == core
                source = jnp.where(is_mine, own22[s, low, :], other22[s, low, :])
                update = source - dot_nt(whole[s, span, :], whole[s])
                owner = (target // 2) % 2
                for b in range(blocks):
                    tile = update[:, b * block : (b + 1) * block]
                    column = maps[s, b]
                    there = pl.ds(pl.multiple_of(column * block, block), block)

                    @pl.when((target < pivot_blocks) & (column < pivot_blocks))
                    def _():
                        pivot_out[owner, :, there] += tile

                    @pl.when((target >= pivot_blocks) & (owner == half))
                    def _():
                        keep_out[:, there] += tile

                    @pl.when((target >= pivot_blocks) & (owner != half))
                    def _():
                        send_out[:, there] += tile


def parent_kernel(place, mine, yours, lower, out, work):
    core, half = place[0], place[2]
    _, rows, pivots = mine.shape
    for h in range(2):
        work[0, pl.ds(pl.multiple_of((2 * h + core) * rows, rows), rows), :] = mine[h]
        work[0, pl.ds(pl.multiple_of((2 * h + 1 - core) * rows, rows), rows), :] = yours[h]
    work[0, pivots:, :] = lower[...]
    factor_panels(work, pivots)
    clear_upper(work, pivots)
    out[0] = work[0, pl.ds(pl.multiple_of((2 * half + core) * rows, rows), rows), :]
    out[1] = work[0, pivots:, :]


def update_kernel(place, base, own, mate, pair, cross, out):
    core, half = place[0], place[2]
    rows = own.shape[0]
    pieces = (
        (own, 2 * half + core),
        (mate, 2 * half + 1 - core),
        (pair, 2 * (1 - half) + core),
        (cross, 2 * (1 - half) + 1 - core),
    )
    for piece, index in pieces:
        side = pl.ds(pl.multiple_of(index * rows, rows), rows)
        out[:, side] = base[:, side] - dot_nt(own[...], piece[...])


def call(kernel, shapes, scratch, scalars, *arrays):
    vmem = pl.BlockSpec(memory_space=pltpu.VMEM)
    smem = pl.BlockSpec(memory_space=pltpu.SMEM)
    many = isinstance(shapes, list)
    made = [jax.ShapeDtypeStruct(s, jnp.float32) for s in (shapes if many else [shapes])]
    return pl.pallas_call(
        kernel,
        out_shape=made if many else made[0],
        in_specs=[smem] * len(scalars) + [vmem] * len(arrays),
        out_specs=[vmem] * len(made) if many else vmem,
        scratch_shapes=[pltpu.VMEM(s, jnp.float32) for s in scratch],
        compiler_params=pltpu.CompilerParams(vmem_limit_bytes=VMEM_LIMIT),
    )(*scalars, *arrays)


def on_device(child_fronts, child_live, row_map, parent_fronts):
    slots, _, quarter, order = child_fronts.shape
    pivots = order // 2
    core = lax.axis_index("front")
    half = lax.axis_index("leaf") % 2
    place = jnp.stack([core, child_live[0], half]).astype(jnp.int32)
    other_core = [(i, i ^ 1) for i in range(lax.axis_size("front"))]
    other_chip = [(i, i ^ 1) for i in range(lax.axis_size("leaf"))]

    def mate(x):
        return lax.ppermute(x, "front", other_core)

    def pair(x):
        return lax.ppermute(x, "leaf", other_chip)

    own_panel = child_fronts[:, :, :, :pivots]
    own22 = child_fronts[:, 1, :, pivots:]
    other_pivot = mate(child_fronts[:, 0, :, :pivots])
    other22 = mate(own22)
    child_panels = call(
        child_kernel,
        (slots, 2, quarter, pivots),
        [(slots, pivots + quarter, pivots)],
        [place],
        own_panel,
        other_pivot,
    )
    own21 = child_panels[:, 1]
    other21 = mate(own21)
    rows, parent_order = parent_fronts.shape[2:]
    parent_pivots = parent_order // 2
    pivot_part, keep, send = call(
        add_kernel,
        [(2, rows, parent_pivots), (rows, parent_order), (rows, parent_order)],
        [(slots, order - pivots, pivots)],
        [place, row_map],
        own22,
        other22,
        own21,
        other21,
        parent_fronts[0],
    )
    pivot_mine = pivot_part + pair(pivot_part)
    pivot_yours = mate(pivot_mine)
    lower = keep + pair(send)
    panel = call(
        parent_kernel,
        (2, rows, parent_pivots),
        [(1, parent_pivots + rows, parent_pivots)],
        [place],
        pivot_mine,
        pivot_yours,
        lower[:, :parent_pivots],
    )
    lower21 = panel[1]
    from_pair = pair(lower21)
    update = call(
        update_kernel,
        (rows, parent_order - parent_pivots),
        [],
        [place],
        lower[:, parent_pivots:],
        lower21,
        mate(lower21),
        from_pair,
        mate(from_pair),
    )
    return child_panels, panel[None], update[None]


def solution(mesh):
    placed = (
        P("leaf", None, "front", None),
        P("leaf"),
        P("leaf", None),
        P("leaf", None, "front", None),
    )
    return jax.shard_map(
        on_device,
        mesh=mesh,
        in_specs=placed,
        out_specs=(
            P("leaf", None, "front", None),
            P("leaf", None, "front", None),
            P("leaf", "front", None),
        ),
        check_vma=False,
    )
```

profile of v0, /device:TPU:0, one launch (start us, length us, event | category | flops | bytes accessed | tf_op | source)
XLA Modules:
  0.0 168.9 jit_solution(1157267347823760972)
XLA Ops:
  0.6 3.5 %slice_bitcast_fusion.1 = (f32[3,256,512]{2,1,0:T(8,128)S(1)}, f32[3,256,512]{2,1,0:T(8,128)}) fusion(f32[3,2,256,1024]{3,2,1,0:T(8,128)} %param.4), kind=kLoop, calls=%fused_computation.1 | loop fusion | bytes 6291456 | tf_op jit(solution)/shard_map/squeeze | solution.py:266
  4.1 0.0 copy-start.1
  4.2 0.5 collective-permute-start
  4.6 0.0 collective-permute-start.1
  4.7 4.1 %slice.21.own = f32[3,2,256,512]{3,2,1,0:T(8,128)} slice(f32[3,2,256,1024]{3,2,1,0:T(8,128)} %param.4), slice={[0:3], [0:2], [0:256], [0:512]} | slice | bytes 6291456 | tf_op jit(solution)/shard_map/slice | solution.py:265
  8.8 0.0 copy-done.1
  9.5 0.6 pad_add_fusion.place
  10.1 0.0 collective-permute-done.other
  10.1 66.7 %shard_map.67 = f32[3,2,256,512]{3,2,1,0:T(8,128)} custom-call(s32[3]{0:T(128)} %pad_add_fusion.place, f32[3,2,256,512]{3,2,1,0:T(8,128)} %slice.21.own, f32[3,256,512]{2,1,0:T(8,128)} %collective-permute-done.other), custom_call_target="tpu_custom_call" | custom-call | tf_op jit(solution)/shard_map/pallas_call | solution.py:240
  76.8 1.5 slice_bitcast_fusion.own21
  78.3 0.0 copy-start
  78.3 0.6 collective-permute-start.2
  78.9 0.0 collective-permute-done.1.other22
  78.9 3.0 %collective-permute-done.2.other21 = f32[3,256,512]{2,1,0:T(8,128)S(1)} collective-permute-done((f32[3,256,512]{2,1,0:T(8,128)S(1)}, f32[3,256,512]{2,1,0:T(8,128)S(1)}, u32[]{:S(2)}, u32[]{:S(2)}) %collective-permute-start.2) | collective-permute-done | bytes 1572896 | tf_op jit(solution)/shard_map/ppermute | solution.py:260
  81.9 0.0 copy-start.3
  81.9 1.1 copy-done.3
  83.0 0.0 copy-done
  83.0 7.3 %shard_map.68 = (f32[2,128,512]{2,1,0:T(8,128)}, f32[128,1024]{1,0:T(8,128)}, f32[128,1024]{1,0:T(8,128)}) custom-call(s32[3]{0:T(128)} %pad_add_fusion.place, s32[3,4]{1,0:T(4,128)} %maps.1, f32[3,256,512]{2,1,0:T(8,128)} %copy-done.1, f32[3,256,512]{2,1,0:T(8,128)} %collective-permute-done.1.other22, f32[3,256,512]{2,1,0:T(8,128)} %copy-done, ...), custom_call_target="tpu_custom_call" | custom-call | tf_op jit(solution)/shard_map/pallas_call | solution.py:240
  90.4 0.0 copy-start.5
  90.4 4.1 %collective-permute-start.3 = (f32[2,128,512]{2,1,0:T(8,128)}, f32[2,128,512]{2,1,0:T(8,128)S(1)}, u32[]{:S(2)}, u32[]{:S(2)}) collective-permute-start(f32[2,128,512]{2,1,0:T(8,128)} %get-tuple-element.6), channel_id=1, source_target_pairs={{0,2},{2,0},{4,6},{6,4},{8,10},{10,8},{12,14},{14,12},{16,18},{18,... | collective-permute-start | bytes 1572872 | tf_op jit(solution)/shard_map/ppermute | solution.py:263
  94.5 0.1 collective-permute-start.5
  94.5 12.1 %collective-permute-done.3 = f32[2,128,512]{2,1,0:T(8,128)S(1)} collective-permute-done((f32[2,128,512]{2,1,0:T(8,128)}, f32[2,128,512]{2,1,0:T(8,128)S(1)}, u32[]{:S(2)}, u32[]{:S(2)}) %collective-permute-start.3) | collective-permute-done | bytes 524320 | tf_op jit(solution)/shard_map/ppermute | solution.py:263
  106.6 1.1 add.11.mine
  107.7 0.0 copy-start.2
  107.7 3.3 %collective-permute-start.4 = (f32[2,128,512]{2,1,0:T(8,128)S(1)}, f32[2,128,512]{2,1,0:T(8,128)S(1)}, u32[]{:S(2)}, u32[]{:S(2)}) collective-permute-start(f32[2,128,512]{2,1,0:T(8,128)S(1)} %add.11.mine), channel_id=1, source_target_pairs={{0,1},{1,0},{2,3},{3,2},{4,5},{5,4},{6,7},{7,6},{8,9},{9,8},{10,11... | collective-permute-start | bytes 1572872 | tf_op jit(solution)/shard_map/ppermute | solution.py:260
  111.0 6.8 %collective-permute-done.5 = f32[128,1024]{1,0:T(8,128)S(1)} collective-permute-done((f32[128,1024]{1,0:T(8,128)}, f32[128,1024]{1,0:T(8,128)S(1)}, u32[]{:S(2)}, u32[]{:S(2)}) %collective-permute-start.5) | collective-permute-done | bytes 524320 | tf_op jit(solution)/shard_map/ppermute | solution.py:263
  117.8 0.0 copy-done.5
  117.8 0.1 add.12
  117.9 0.8 fusion
  118.7 0.0 collective-permute-done.4.yours
  118.7 0.0 copy-start.6
  118.7 0.0 copy-done.2
  118.7 0.8 copy-done.6
  119.5 34.0 %shard_map.69 = f32[2,128,512]{2,1,0:T(8,128)} custom-call(s32[3]{0:T(128)} %pad_add_fusion.place, f32[2,128,512]{2,1,0:T(8,128)} %copy-done.2, f32[2,128,512]{2,1,0:T(8,128)} %copy-done.6, f32[128,512]{1,0:T(8,128)} %get-tuple-element.12.lower), custom_call_target="tpu_custom_call" | custom-call | tf_op jit(solution)/shard_map/pallas_call | solution.py:240
  153.5 1.0 slice_bitcast_fusion.3.own
  154.5 0.0 copy-start.4
  154.5 2.4 %collective-permute-start.7 = (f32[128,512]{1,0:T(8,128)S(1)}, f32[128,512]{1,0:T(8,128)S(1)}, u32[]{:S(2)}, u32[]{:S(2)}) collective-permute-start(f32[128,512]{1,0:T(8,128)S(1)} %slice_bitcast_fusion.3.own), channel_id=1, source_target_pairs={{0,2},{2,0},{4,6},{6,4},{8,10},{10,8},{12,14},{14,12},{16,18},{18,... | collective-permute-start | bytes 786440 | tf_op jit(solution)/shard_map/ppermute | solution.py:263
  156.9 0.0 collective-permute-start.6
  157.0 6.8 %collective-permute-done.7.pair = f32[128,512]{1,0:T(8,128)S(1)} collective-permute-done((f32[128,512]{1,0:T(8,128)S(1)}, f32[128,512]{1,0:T(8,128)S(1)}, u32[]{:S(2)}, u32[]{:S(2)}) %collective-permute-start.7) | collective-permute-done | bytes 262176 | tf_op jit(solution)/shard_map/ppermute | solution.py:263
  163.7 0.0 collective-permute-start.8
  163.7 0.0 collective-permute-done.6.mate
  163.7 0.0 copy-start.8
  163.7 1.5 collective-permute-done.8.cross
  165.2 0.0 copy-done.4
  165.2 0.0 copy-done.7
  165.2 0.0 copy-done.8
  165.3 0.7 copy-done.9
  165.9 3.0 %shard_map.70 = f32[128,512]{1,0:T(8,128)} custom-call(s32[3]{0:T(128)} %pad_add_fusion.place, f32[128,512]{1,0:T(8,128)} %get-tuple-element.11.base, f32[128,512]{1,0:T(8,128)} %copy-done.4, f32[128,512]{1,0:T(8,128)} %copy-done.8, f32[128,512]{1,0:T(8,128)} %copy-done.7, f32[128,512]{1,0:T(8,128)} %copy-done.9), custom_call_target="tpu_custom_call" | custom-call | tf_op jit(solution)/shard_map/pallas_call | solution.py:240
  (2 shorter events, 0.0 us)
Async XLA Ops:
  4.1 4.7 %copy-start.1 = (f32[3,256,512]{2,1,0:T(8,128)}, f32[3,256,512]{2,1,0:T(8,128)S(1)}, u32[]{:S(2)}) copy-start(f32[3,256,512]{2,1,0:T(8,128)S(1)} %get-tuple-element.9.own22) | copy-start | bytes 4718596
  4.2 5.9 %collective-permute-start = (f32[3,256,512]{2,1,0:T(8,128)}, f32[3,256,512]{2,1,0:T(8,128)}, u32[]{:S(2)}, u32[]{:S(2)}) collective-permute-start(f32[3,256,512]{2,1,0:T(8,128)} %get-tuple-element.10), channel_id=1, source_target_pairs={{0,1},{1,0},{2,3},{3,2},{4,5},{5,4},{6,7},{7,6},{8,9},{9,8},{10,11... | collective-permute-start | bytes 4718600 | tf_op jit(solution)/shard_map/ppermute | solution.py:260
  4.6 74.2 %collective-permute-start.1 = (f32[3,256,512]{2,1,0:T(8,128)S(1)}, f32[3,256,512]{2,1,0:T(8,128)}, u32[]{:S(2)}, u32[]{:S(2)}) collective-permute-start(f32[3,256,512]{2,1,0:T(8,128)S(1)} %get-tuple-element.9.own22), channel_id=1, source_target_pairs={{0,1},{1,0},{2,3},{3,2},{4,5},{5,4},{6,7},{7,6},{8,9},{9,8},{10,11... | collective-permute-start | bytes 4718600 | tf_op jit(solution)/shard_map/ppermute | solution.py:260
  78.3 4.7 %copy-start = (f32[3,256,512]{2,1,0:T(8,128)}, f32[3,256,512]{2,1,0:T(8,128)S(1)}, u32[]{:S(2)}) copy-start(f32[3,256,512]{2,1,0:T(8,128)S(1)} %slice_bitcast_fusion.own21) | copy-start | bytes 4718596
  78.3 3.6 %collective-permute-start.2 = (f32[3,256,512]{2,1,0:T(8,128)S(1)}, f32[3,256,512]{2,1,0:T(8,128)S(1)}, u32[]{:S(2)}, u32[]{:S(2)}) collective-permute-start(f32[3,256,512]{2,1,0:T(8,128)S(1)} %slice_bitcast_fusion.own21), channel_id=1, source_target_pairs={{0,1},{1,0},{2,3},{3,2},{4,5},{5,4},{6,7},{7,6},{8,9},{9,8},{10,11... | collective-permute-start | bytes 4718600 | tf_op jit(solution)/shard_map/ppermute | solution.py:260
  81.9 1.1 copy-start.3
  90.4 27.5 %copy-start.5 = (f32[128,1024]{1,0:T(8,128)S(1)}, f32[128,1024]{1,0:T(8,128)}, u32[]{:S(2)}) copy-start(f32[128,1024]{1,0:T(8,128)} %get-tuple-element.7) | copy-start | bytes 1572868
  90.4 16.2 %collective-permute-start.3 = (f32[2,128,512]{2,1,0:T(8,128)}, f32[2,128,512]{2,1,0:T(8,128)S(1)}, u32[]{:S(2)}, u32[]{:S(2)}) collective-permute-start(f32[2,128,512]{2,1,0:T(8,128)} %get-tuple-element.6), channel_id=1, source_target_pairs={{0,2},{2,0},{4,6},{6,4},{8,10},{10,8},{12,14},{14,12},{16,18},{18,... | collective-permute-start | bytes 1572872 | tf_op jit(solution)/shard_map/ppermute | solution.py:263
  94.5 23.4 %collective-permute-start.5 = (f32[128,1024]{1,0:T(8,128)}, f32[128,1024]{1,0:T(8,128)S(1)}, u32[]{:S(2)}, u32[]{:S(2)}) collective-permute-start(f32[128,1024]{1,0:T(8,128)} %get-tuple-element.8), channel_id=1, source_target_pairs={{0,2},{2,0},{4,6},{6,4},{8,10},{10,8},{12,14},{14,12},{16,18},{18,... | collective-permute-start | bytes 1572872 | tf_op jit(solution)/shard_map/ppermute | solution.py:263
  107.7 11.0 %copy-start.2 = (f32[2,128,512]{2,1,0:T(8,128)}, f32[2,128,512]{2,1,0:T(8,128)S(1)}, u32[]{:S(2)}) copy-start(f32[2,128,512]{2,1,0:T(8,128)S(1)} %add.11.mine) | copy-start | bytes 1572868
  107.7 11.0 %collective-permute-start.4 = (f32[2,128,512]{2,1,0:T(8,128)S(1)}, f32[2,128,512]{2,1,0:T(8,128)S(1)}, u32[]{:S(2)}, u32[]{:S(2)}) collective-permute-start(f32[2,128,512]{2,1,0:T(8,128)S(1)} %add.11.mine), channel_id=1, source_target_pairs={{0,1},{1,0},{2,3},{3,2},{4,5},{5,4},{6,7},{7,6},{8,9},{9,8},{10,11... | collective-permute-start | bytes 1572872 | tf_op jit(solution)/shard_map/ppermute | solution.py:260
  118.7 0.8 copy-start.6
  154.5 10.8 %copy-start.4 = (f32[128,512]{1,0:T(8,128)}, f32[128,512]{1,0:T(8,128)S(1)}, u32[]{:S(2)}) copy-start(f32[128,512]{1,0:T(8,128)S(1)} %slice_bitcast_fusion.3.own) | copy-start | bytes 786436
  154.5 9.2 %collective-permute-start.7 = (f32[128,512]{1,0:T(8,128)S(1)}, f32[128,512]{1,0:T(8,128)S(1)}, u32[]{:S(2)}, u32[]{:S(2)}) collective-permute-start(f32[128,512]{1,0:T(8,128)S(1)} %slice_bitcast_fusion.3.own), channel_id=1, source_target_pairs={{0,2},{2,0},{4,6},{6,4},{8,10},{10,8},{12,14},{14,12},{16,18},{18,... | collective-permute-start | bytes 786440 | tf_op jit(solution)/shard_map/ppermute | solution.py:263
  156.9 6.8 %collective-permute-start.6 = (f32[128,512]{1,0:T(8,128)S(1)}, f32[128,512]{1,0:T(8,128)S(1)}, u32[]{:S(2)}, u32[]{:S(2)}) collective-permute-start(f32[128,512]{1,0:T(8,128)S(1)} %slice_bitcast_fusion.3.own), channel_id=1, source_target_pairs={{0,1},{1,0},{2,3},{3,2},{4,5},{5,4},{6,7},{7,6},{8,9},{9,8},{10,11... | collective-permute-start | bytes 786440 | tf_op jit(solution)/shard_map/ppermute | solution.py:260
  163.7 1.5 copy-start.7
  163.7 1.5 collective-permute-start.8
  163.7 1.5 copy-start.8
  165.2 0.7 copy-start.9
where the time goes:
time: 171 us; the launch traced here: 169 us
  Pallas kernels  111 us (65%)
  waiting for transfers between devices  30.2 us (18%)
  local copies, waits for them, and re-layouts  13.6 us (8%)
  starting transfers between devices  11 us (6%)
  other arithmetic  1.77 us (1%)
    pallas_call x4, Pallas kernels, call(): pl.pallas_call(kernel, out_shape=made if many else made[0], in_specs=[sme...  111 us
    ppermute x3, waiting for transfers between devices, pair(): return lax.ppermute(x, 'leaf', other_chip)  25.6 us
    ppermute x3, starting transfers between devices, pair(): return lax.ppermute(x, 'leaf', other_chip)  6.6 us
    ppermute x6, waiting for transfers between devices, mate(): return lax.ppermute(x, 'front', other_core)  4.56 us
    ppermute x6, starting transfers between devices, mate(): return lax.ppermute(x, 'front', other_core)  4.39 us
    slice x1, local copies, waits for them, and re-layouts, on_device(): own_panel = child_fronts[:, :, :, :pivots]  4.15 us
    squeeze x1, local copies, waits for them, and re-layouts, on_device(): own22 = child_fronts[:, 1, :, pivots:]  3.52 us
  transfers between devices with their start and end apart: 9, of which 5 were waited for; matrix products, arithmetic and copies ran while one was open for 5% of the time, Pallas kernels for 39%

commit v1 on v0

--- a/solution.py
+++ b/solution.py
@@ -7,35 +7,45 @@
 from jax.experimental.pallas import tpu as pltpu
 from jax.sharding import PartitionSpec as P
 
-HIGHEST = lax.Precision.HIGHEST
 LANES = 128
 SUB = 8
 GROUP = 4
 VMEM_LIMIT = 60 * 1024 * 1024
 
 
+def split(x):
+    high = x.astype(jnp.bfloat16)
+    return high, (x - high.astype(jnp.float32)).astype(jnp.bfloat16)
+
+
 def dot_nt(a, b):
+    a_high, a_low = split(a)
+    b_high, b_low = split(b)
     return lax.dot_general(
-        a, b, (((1,), (1,)), ((), ())), precision=HIGHEST, preferred_element_type=jnp.float32
+        jnp.concatenate([a_high, a_high, a_low], axis=1),
+        jnp.concatenate([b_high, b_low, b_high], axis=1),
+        (((1,), (1,)), ((), ())),
+        preferred_element_type=jnp.float32,
     )
 
 
 def spread_lane(x, lane):
-    return jnp.broadcast_to(x[:, lane : lane + 1], (SUB, LANES))
+    return jnp.take_along_axis(x, jnp.full((SUB, LANES), lane, jnp.int32), 1, mode="promise_in_bounds")
 
 
 def spread_row(x, row):
-    return jnp.broadcast_to(x[row : row + 1, :], (SUB, LANES))
+    return jnp.take_along_axis(x, jnp.full((SUB, LANES), row, jnp.int32), 0, mode="promise_in_bounds")
 
 
 def eliminate_group(tiles, start, lane_ids, row_ids):
     tile, first = divmod(start, SUB)
     size = GROUP
     rows = [spread_row(tiles[tile], first + k) for k in range(size)]
+    heads = [spread_lane(tiles[tile], start + k) for k in range(size)]
     entry = {}
     for k in range(size):
         for l in range(k + 1):
-            entry[k, l] = spread_lane(rows[k], start + l)
+            entry[k, l] = spread_row(heads[l], first + k)
     ratio = {}
     inverse = []
     for k in range(size):
@@ -52,24 +62,20 @@
     for k in range(size):
         for l in range(k):
             rows[k] = rows[k] - ratio[k, l] * rows[l]
-    scaled = [rows[k] * inverse[k] for k in range(size)]
+    solved = [rows[k] * inverse[k] for k in range(size)]
+    for k in range(size - 2, -1, -1):
+        for m in range(k + 1, size):
+            solved[k] = solved[k] - ratio[m, k] * solved[m]
     result = list(tiles)
     for t in range(tile, len(tiles)):
         old = tiles[t]
         if t == tile and first + size == SUB:
             new = old
         else:
-            factors = []
+            factors = [heads[k] if t == tile else spread_lane(old, start + k) for k in range(size)]
+            new = jnp.where(inside, 0.0, old)
             for k in range(size):
-                value = spread_lane(old, start + k)
-                for l in range(k):
-                    value = value - factors[l] * ratio[k, l]
-                factors.append(value)
-            new = jnp.where(inside, 0.0, old)
-            total = factors[0] * scaled[0]
-            for k in range(1, size):
-                total = total + factors[k] * scaled[k]
-            new = new - total
+                new = new - factors[k] * solved[k]
         if t == tile:
             new = jnp.where(row_ids < first, old, new)
             for k in range(size):
@@ -91,8 +97,8 @@
     return [jnp.where(columns <= rows, jnp.concatenate(t, axis=0), 0.0) for t in tiles]
 
 
-def factor_panels(work, pivots):
-    fronts, rows, _ = work.shape
+def factor_pivots(work, saved):
+    fronts, pivots, _ = work.shape
     steps = pivots // LANES
     triangle = lax.broadcasted_iota(jnp.int32, (LANES, LANES), 1) <= lax.broadcasted_iota(
         jnp.int32, (LANES, LANES), 0
@@ -100,32 +106,42 @@
 
     @pl.loop(0, steps)
     def _(step):
-        here = pl.multiple_of(step * LANES, LANES)
-        span = pl.ds(here, LANES)
+        span = pl.ds(pl.multiple_of(step * LANES, LANES), LANES)
         inverses = factor_inverses([work[f, span, span] for f in range(fronts)])
         for f in range(fronts):
+            saved[f, step] = inverses[f]
             work[f, span, span] = jnp.where(
                 triangle, dot_nt(work[f, span, span], inverses[f]), 0.0
             )
 
-        @pl.loop(step + 1, rows // LANES)
+        @pl.loop(step + 1, steps)
         def _(below):
             low = pl.ds(pl.multiple_of(below * LANES, LANES), LANES)
             for f in range(fronts):
-                work[f, low, span] = dot_nt(work[f, low, span], inverses[f])
+                work[f, low, span] = dot_nt(work[f, low, span], saved[f, step])
 
         @pl.loop(step + 1, steps)
         def _(column):
             side = pl.ds(pl.multiple_of(column * LANES, LANES), LANES)
-            others = [work[f, side, span] for f in range(fronts)]
-
-            @pl.loop(column, rows // LANES)
+
+            @pl.loop(column, steps)
             def _(below):
                 low = pl.ds(pl.multiple_of(below * LANES, LANES), LANES)
                 for f in range(fronts):
                     work[f, low, side] = work[f, low, side] - dot_nt(
-                        work[f, low, span], others[f]
+                        work[f, low, span], work[f, side, span]
                     )
+
+
+def solve_rows(work, saved, lower):
+    fronts, pivots, _ = work.shape
+    for step in range(pivots // LANES):
+        top = step * LANES
+        for f in range(fronts):
+            value = lower[f][:, top : top + LANES]
+            if step:
+                value = value - dot_nt(lower[f][:, :top], work[f, top : top + LANES, :top])
+            lower[f][:, top : top + LANES] = dot_nt(value, saved[f, step])
 
 
 def clear_upper(work, pivots):
@@ -138,7 +154,7 @@
                 )
 
 
-def child_kernel(place, own, other, out, work):
+def child_kernel(place, own, other, out, work, saved):
     core, live = place[0], place[1]
     slots, _, half, pivots = own.shape
     mine = pl.ds(pl.multiple_of(core * half, half), half)
@@ -146,12 +162,13 @@
     for s in range(slots):
         work[s, mine, :] = own[s, 0]
         work[s, yours, :] = other[s]
-        work[s, 2 * half :, :] = own[s, 1]
-    factor_panels(work, pivots)
+        out[s, 1] = own[s, 1]
+    factor_pivots(work, saved)
     clear_upper(work, pivots)
+    solve_rows(work, saved, [out.at[s, 1] for s in range(slots)])
     for s in range(slots):
         out[s, 0] = jnp.where(s < live, work[s, mine, :], 0.0)
-        out[s, 1] = jnp.where(s < live, work[s, 2 * half :, :], 0.0)
+        out[s, 1] = jnp.where(s < live, out[s, 1], 0.0)
 
 
 def add_kernel(
@@ -205,17 +222,17 @@
                         send_out[:, there] += tile
 
 
-def parent_kernel(place, mine, yours, lower, out, work):
+def parent_kernel(place, mine, yours, lower, out, work, saved):
     core, half = place[0], place[2]
     _, rows, pivots = mine.shape
     for h in range(2):
         work[0, pl.ds(pl.multiple_of((2 * h + core) * rows, rows), rows), :] = mine[h]
         work[0, pl.ds(pl.multiple_of((2 * h + 1 - core) * rows, rows), rows), :] = yours[h]
-    work[0, pivots:, :] = lower[...]
-    factor_panels(work, pivots)
+    out[1] = lower[...]
+    factor_pivots(work, saved)
     clear_upper(work, pivots)
+    solve_rows(work, saved, [out.at[1]])
     out[0] = work[0, pl.ds(pl.multiple_of((2 * half + core) * rows, rows), rows), :]
-    out[1] = work[0, pivots:, :]
 
 
 def update_kernel(place, base, own, mate, pair, cross, out):
@@ -269,7 +286,7 @@
     child_panels = call(
         child_kernel,
         (slots, 2, quarter, pivots),
-        [(slots, pivots + quarter, pivots)],
+        [(slots, pivots, pivots), (slots, pivots // LANES, LANES, LANES)],
         [place],
         own_panel,
         other_pivot,
@@ -295,7 +312,7 @@
     panel = call(
         parent_kernel,
         (2, rows, parent_pivots),
-        [(1, parent_pivots + rows, parent_pivots)],
+        [(1, parent_pivots, parent_pivots), (1, parent_pivots // LANES, LANES, LANES)],
         [place],
         pivot_mine,
         pivot_yours,

time: 171 us -> 138 us (0.81); the launches traced: 169 us -> 138 us
  Pallas kernels: 111 us -> 79.1 us
  waiting for transfers between devices: 30.2 us -> 32.9 us
    pallas_call x4, Pallas kernels: 111 us -> 79.1 us  [call(): pl.pallas_call(kernel, out_shape=made if many else made[0], in_specs=[sme...]
    ppermute x6, starting transfers between devices: 4.39 us -> 1.14 us  [mate(): return lax.ppermute(x, 'front', other_core)]
    ppermute x3, waiting for transfers between devices: 25.6 us -> 28.4 us  [pair(): return lax.ppermute(x, 'leaf', other_chip)]
    ppermute x3, starting transfers between devices: 6.6 us -> 8.42 us  [pair(): return lax.ppermute(x, 'leaf', other_chip)]
  transfers between devices with their start and end apart: 9 -> 9, of which waited for: 5 -> 5; matrix products, arithmetic and copies ran while one was open for 5% -> 6% of each run, Pallas kernels for 39% -> 32%
where the time goes in v1:
time: 138 us
  Pallas kernels  79.1 us (57%)
  waiting for transfers between devices  32.9 us (24%)
  local copies, waits for them, and re-layouts  13.6 us (10%)
  starting transfers between devices  9.56 us (7%)
  other arithmetic  1.77 us (1%)
    pallas_call x4, Pallas kernels, call(): pl.pallas_call(kernel, out_shape=made if many else made[0], in_specs=[sme...  79.1 us
    ppermute x3, waiting for transfers between devices, pair(): return lax.ppermute(x, 'leaf', other_chip)  28.4 us
    ppermute x3, starting transfers between devices, pair(): return lax.ppermute(x, 'leaf', other_chip)  8.42 us
    ppermute x6, waiting for transfers between devices, mate(): return lax.ppermute(x, 'front', other_core)  4.56 us
    slice x1, local copies, waits for them, and re-layouts, on_device(): own_panel = child_fronts[:, :, :, :pivots]  4.15 us
    squeeze x1, local copies, waits for them, and re-layouts, on_device(): own22 = child_fronts[:, 1, :, pivots:]  3.52 us
  transfers between devices with their start and end apart: 9, of which 5 were waited for; matrix products, arithmetic and copies ran while one was open for 6% of the time, Pallas kernels for 32%

profile of v1, /device:TPU:0, one launch (start us, length us, event | category | flops | bytes accessed | tf_op | source)
XLA Modules:
  0.0 138.3 jit_solution(15841456505407868874)
XLA Ops:
  0.6 3.5 %slice_bitcast_fusion.1 = (f32[3,256,512]{2,1,0:T(8,128)S(1)}, f32[3,256,512]{2,1,0:T(8,128)}) fusion(f32[3,2,256,1024]{3,2,1,0:T(8,128)} %param.4), kind=kLoop, calls=%fused_computation.1 | loop fusion | bytes 6291456 | tf_op jit(solution)/shard_map/squeeze | solution.py:283
  4.1 0.0 copy-start.1
  4.2 0.5 collective-permute-start
  4.6 0.0 collective-permute-start.1
  4.7 4.1 %slice.21.own = f32[3,2,256,512]{3,2,1,0:T(8,128)} slice(f32[3,2,256,1024]{3,2,1,0:T(8,128)} %param.4), slice={[0:3], [0:2], [0:256], [0:512]} | slice | bytes 6291456 | tf_op jit(solution)/shard_map/slice | solution.py:282
  8.8 0.0 copy-done.1
  9.5 0.6 pad_add_fusion.place
  10.1 0.0 collective-permute-done.other
  10.1 44.1 %shard_map.67 = f32[3,2,256,512]{3,2,1,0:T(8,128)} custom-call(s32[3]{0:T(128)} %pad_add_fusion.place, f32[3,2,256,512]{3,2,1,0:T(8,128)} %slice.21.own, f32[3,256,512]{2,1,0:T(8,128)} %collective-permute-done.other), custom_call_target="tpu_custom_call" | custom-call | tf_op jit(solution)/shard_map/pallas_call | solution.py:257
  54.1 1.5 %slice_bitcast_fusion.own21 = f32[3,256,512]{2,1,0:T(8,128)S(1)} fusion(f32[3,2,256,512]{3,2,1,0:T(8,128)} %shard_map.67), kind=kLoop, calls=%fused_computation | loop fusion | bytes 3145728 | tf_op jit(solution)/shard_map/squeeze | solution.py:294
  55.7 0.0 copy-start
  55.7 0.6 collective-permute-start.2
  56.2 0.0 collective-permute-done.1.other22
  56.2 3.0 %collective-permute-done.2.other21 = f32[3,256,512]{2,1,0:T(8,128)S(1)} collective-permute-done((f32[3,256,512]{2,1,0:T(8,128)S(1)}, f32[3,256,512]{2,1,0:T(8,128)S(1)}, u32[]{:S(2)}, u32[]{:S(2)}) %collective-permute-start.2) | collective-permute-done | bytes 1572896 | tf_op jit(solution)/shard_map/ppermute | solution.py:277
  59.3 0.0 copy-start.3
  59.3 1.1 copy-done.3
  60.4 0.0 copy-done
  60.4 5.6 %shard_map.68 = (f32[2,128,512]{2,1,0:T(8,128)}, f32[128,1024]{1,0:T(8,128)}, f32[128,1024]{1,0:T(8,128)}) custom-call(s32[3]{0:T(128)} %pad_add_fusion.place, s32[3,4]{1,0:T(4,128)} %maps.1, f32[3,256,512]{2,1,0:T(8,128)} %copy-done.1, f32[3,256,512]{2,1,0:T(8,128)} %collective-permute-done.1.other22, f32[3,256,512]{2,1,0:T(8,128)} %copy-done, ...), custom_call_target="tpu_custom_call" | custom-call | tf_op jit(solution)/shard_map/pallas_call | solution.py:257
  66.0 0.0 copy-start.5
  66.0 6.5 %collective-permute-start.3 = (f32[2,128,512]{2,1,0:T(8,128)}, f32[2,128,512]{2,1,0:T(8,128)S(1)}, u32[]{:S(2)}, u32[]{:S(2)}) collective-permute-start(f32[2,128,512]{2,1,0:T(8,128)} %get-tuple-element.6), channel_id=1, source_target_pairs={{0,2},{2,0},{4,6},{6,4},{8,10},{10,8},{12,14},{14,12},{16,18},{18,... | collective-permute-start | bytes 1572872 | tf_op jit(solution)/shard_map/ppermute | solution.py:280
  72.5 0.1 collective-permute-start.5
  72.6 12.9 %collective-permute-done.3 = f32[2,128,512]{2,1,0:T(8,128)S(1)} collective-permute-done((f32[2,128,512]{2,1,0:T(8,128)}, f32[2,128,512]{2,1,0:T(8,128)S(1)}, u32[]{:S(2)}, u32[]{:S(2)}) %collective-permute-start.3) | collective-permute-done | bytes 524320 | tf_op jit(solution)/shard_map/ppermute | solution.py:280
  85.5 1.1 add.11.mine
  86.6 0.0 copy-start.2
  86.6 0.1 collective-permute-start.4
  86.7 9.5 %collective-permute-done.5 = f32[128,1024]{1,0:T(8,128)S(1)} collective-permute-done((f32[128,1024]{1,0:T(8,128)}, f32[128,1024]{1,0:T(8,128)S(1)}, u32[]{:S(2)}, u32[]{:S(2)}) %collective-permute-start.5) | collective-permute-done | bytes 524320 | tf_op jit(solution)/shard_map/ppermute | solution.py:280
  96.2 0.0 copy-done.5
  96.2 0.1 add.12
  96.2 0.8 fusion
  97.0 0.0 collective-permute-done.4.yours
  97.1 0.0 copy-start.6
  97.1 0.0 copy-done.2
  97.1 0.8 copy-done.6
  97.8 26.9 %shard_map.69 = f32[2,128,512]{2,1,0:T(8,128)} custom-call(s32[3]{0:T(128)} %pad_add_fusion.place, f32[2,128,512]{2,1,0:T(8,128)} %copy-done.2, f32[2,128,512]{2,1,0:T(8,128)} %copy-done.6, f32[128,512]{1,0:T(8,128)} %get-tuple-element.12.lower), custom_call_target="tpu_custom_call" | custom-call | tf_op jit(solution)/shard_map/pallas_call | solution.py:257
  124.7 1.0 slice_bitcast_fusion.3.own
  125.7 0.0 copy-start.4
  125.7 1.8 %collective-permute-start.7 = (f32[128,512]{1,0:T(8,128)S(1)}, f32[128,512]{1,0:T(8,128)S(1)}, u32[]{:S(2)}, u32[]{:S(2)}) collective-permute-start(f32[128,512]{1,0:T(8,128)S(1)} %slice_bitcast_fusion.3.own), channel_id=1, source_target_pairs={{0,2},{2,0},{4,6},{6,4},{8,10},{10,8},{12,14},{14,12},{16,18},{18,... | collective-permute-start | bytes 786440 | tf_op jit(solution)/shard_map/ppermute | solution.py:280
  127.5 0.0 collective-permute-start.6
  127.5 6.0 %collective-permute-done.7.pair = f32[128,512]{1,0:T(8,128)S(1)} collective-permute-done((f32[128,512]{1,0:T(8,128)S(1)}, f32[128,512]{1,0:T(8,128)S(1)}, u32[]{:S(2)}, u32[]{:S(2)}) %collective-permute-start.7) | collective-permute-done | bytes 262176 | tf_op jit(solution)/shard_map/ppermute | solution.py:280
  133.5 0.0 collective-permute-start.8
  133.6 0.0 collective-permute-done.6.mate
  133.6 0.0 copy-start.8
  133.6 1.5 %collective-permute-done.8.cross = f32[128,512]{1,0:T(8,128)S(1)} collective-permute-done((f32[128,512]{1,0:T(8,128)S(1)}, f32[128,512]{1,0:T(8,128)S(1)}, u32[]{:S(2)}, u32[]{:S(2)}) %collective-permute-start.8) | collective-permute-done | bytes 262176 | tf_op jit(solution)/shard_map/ppermute | solution.py:277
  135.1 0.0 copy-done.4
  135.1 0.0 copy-done.7
  135.1 0.0 copy-done.8
  135.1 0.7 copy-done.9
  135.8 2.6 %shard_map.70 = f32[128,512]{1,0:T(8,128)} custom-call(s32[3]{0:T(128)} %pad_add_fusion.place, f32[128,512]{1,0:T(8,128)} %get-tuple-element.11.base, f32[128,512]{1,0:T(8,128)} %copy-done.4, f32[128,512]{1,0:T(8,128)} %copy-done.8, f32[128,512]{1,0:T(8,128)} %copy-done.7, f32[128,512]{1,0:T(8,128)} %copy-done.9), custom_call_target="tpu_custom_call" | custom-call | tf_op jit(solution)/shard_map/pallas_call | solution.py:257
  (2 shorter events, 0.0 us)
Async XLA Ops:
  4.1 4.7 %copy-start.1 = (f32[3,256,512]{2,1,0:T(8,128)}, f32[3,256,512]{2,1,0:T(8,128)S(1)}, u32[]{:S(2)}) copy-start(f32[3,256,512]{2,1,0:T(8,128)S(1)} %get-tuple-element.9.own22) | copy-start | bytes 4718596
  4.2 5.9 %collective-permute-start = (f32[3,256,512]{2,1,0:T(8,128)}, f32[3,256,512]{2,1,0:T(8,128)}, u32[]{:S(2)}, u32[]{:S(2)}) collective-permute-start(f32[3,256,512]{2,1,0:T(8,128)} %get-tuple-element.10), channel_id=1, source_target_pairs={{0,1},{1,0},{2,3},{3,2},{4,5},{5,4},{6,7},{7,6},{8,9},{9,8},{10,11... | collective-permute-start | bytes 4718600 | tf_op jit(solution)/shard_map/ppermute | solution.py:277
  4.6 51.6 %collective-permute-start.1 = (f32[3,256,512]{2,1,0:T(8,128)S(1)}, f32[3,256,512]{2,1,0:T(8,128)}, u32[]{:S(2)}, u32[]{:S(2)}) collective-permute-start(f32[3,256,512]{2,1,0:T(8,128)S(1)} %get-tuple-element.9.own22), channel_id=1, source_target_pairs={{0,1},{1,0},{2,3},{3,2},{4,5},{5,4},{6,7},{7,6},{8,9},{9,8},{10,11... | collective-permute-start | bytes 4718600 | tf_op jit(solution)/shard_map/ppermute | solution.py:277
  55.7 4.7 %copy-start = (f32[3,256,512]{2,1,0:T(8,128)}, f32[3,256,512]{2,1,0:T(8,128)S(1)}, u32[]{:S(2)}) copy-start(f32[3,256,512]{2,1,0:T(8,128)S(1)} %slice_bitcast_fusion.own21) | copy-start | bytes 4718596
  55.7 3.6 %collective-permute-start.2 = (f32[3,256,512]{2,1,0:T(8,128)S(1)}, f32[3,256,512]{2,1,0:T(8,128)S(1)}, u32[]{:S(2)}, u32[]{:S(2)}) collective-permute-start(f32[3,256,512]{2,1,0:T(8,128)S(1)} %slice_bitcast_fusion.own21), channel_id=1, source_target_pairs={{0,1},{1,0},{2,3},{3,2},{4,5},{5,4},{6,7},{7,6},{8,9},{9,8},{10,11... | collective-permute-start | bytes 4718600 | tf_op jit(solution)/shard_map/ppermute | solution.py:277
  59.3 1.1 copy-start.3
  66.0 30.2 %copy-start.5 = (f32[128,1024]{1,0:T(8,128)S(1)}, f32[128,1024]{1,0:T(8,128)}, u32[]{:S(2)}) copy-start(f32[128,1024]{1,0:T(8,128)} %get-tuple-element.7) | copy-start | bytes 1572868
  66.0 19.5 %collective-permute-start.3 = (f32[2,128,512]{2,1,0:T(8,128)}, f32[2,128,512]{2,1,0:T(8,128)S(1)}, u32[]{:S(2)}, u32[]{:S(2)}) collective-permute-start(f32[2,128,512]{2,1,0:T(8,128)} %get-tuple-element.6), channel_id=1, source_target_pairs={{0,2},{2,0},{4,6},{6,4},{8,10},{10,8},{12,14},{14,12},{16,18},{18,... | collective-permute-start | bytes 1572872 | tf_op jit(solution)/shard_map/ppermute | solution.py:280
  72.5 23.7 %collective-permute-start.5 = (f32[128,1024]{1,0:T(8,128)}, f32[128,1024]{1,0:T(8,128)S(1)}, u32[]{:S(2)}, u32[]{:S(2)}) collective-permute-start(f32[128,1024]{1,0:T(8,128)} %get-tuple-element.8), channel_id=1, source_target_pairs={{0,2},{2,0},{4,6},{6,4},{8,10},{10,8},{12,14},{14,12},{16,18},{18,... | collective-permute-start | bytes 1572872 | tf_op jit(solution)/shard_map/ppermute | solution.py:280
  86.6 10.5 %copy-start.2 = (f32[2,128,512]{2,1,0:T(8,128)}, f32[2,128,512]{2,1,0:T(8,128)S(1)}, u32[]{:S(2)}) copy-start(f32[2,128,512]{2,1,0:T(8,128)S(1)} %add.11.mine) | copy-start | bytes 1572868
  86.6 10.4 %collective-permute-start.4 = (f32[2,128,512]{2,1,0:T(8,128)S(1)}, f32[2,128,512]{2,1,0:T(8,128)S(1)}, u32[]{:S(2)}, u32[]{:S(2)}) collective-permute-start(f32[2,128,512]{2,1,0:T(8,128)S(1)} %add.11.mine), channel_id=1, source_target_pairs={{0,1},{1,0},{2,3},{3,2},{4,5},{5,4},{6,7},{7,6},{8,9},{9,8},{10,11... | collective-permute-start | bytes 1572872 | tf_op jit(solution)/shard_map/ppermute | solution.py:277
  97.1 0.8 copy-start.6
  125.7 9.4 %copy-start.4 = (f32[128,512]{1,0:T(8,128)}, f32[128,512]{1,0:T(8,128)S(1)}, u32[]{:S(2)}) copy-start(f32[128,512]{1,0:T(8,128)S(1)} %slice_bitcast_fusion.3.own) | copy-start | bytes 786436
  125.7 7.8 %collective-permute-start.7 = (f32[128,512]{1,0:T(8,128)S(1)}, f32[128,512]{1,0:T(8,128)S(1)}, u32[]{:S(2)}, u32[]{:S(2)}) collective-permute-start(f32[128,512]{1,0:T(8,128)S(1)} %slice_bitcast_fusion.3.own), channel_id=1, source_target_pairs={{0,2},{2,0},{4,6},{6,4},{8,10},{10,8},{12,14},{14,12},{16,18},{18,... | collective-permute-start | bytes 786440 | tf_op jit(solution)/shard_map/ppermute | solution.py:280
  127.5 6.0 %collective-permute-start.6 = (f32[128,512]{1,0:T(8,128)S(1)}, f32[128,512]{1,0:T(8,128)S(1)}, u32[]{:S(2)}, u32[]{:S(2)}) collective-permute-start(f32[128,512]{1,0:T(8,128)S(1)} %slice_bitcast_fusion.3.own), channel_id=1, source_target_pairs={{0,1},{1,0},{2,3},{3,2},{4,5},{5,4},{6,7},{7,6},{8,9},{9,8},{10,11... | collective-permute-start | bytes 786440 | tf_op jit(solution)/shard_map/ppermute | solution.py:277
  133.5 1.5 %copy-start.7 = (f32[128,512]{1,0:T(8,128)}, f32[128,512]{1,0:T(8,128)S(1)}, u32[]{:S(2)}) copy-start(f32[128,512]{1,0:T(8,128)S(1)} %collective-permute-done.7.pair) | copy-start | bytes 786436
  133.5 1.5 %collective-permute-start.8 = (f32[128,512]{1,0:T(8,128)S(1)}, f32[128,512]{1,0:T(8,128)S(1)}, u32[]{:S(2)}, u32[]{:S(2)}) collective-permute-start(f32[128,512]{1,0:T(8,128)S(1)} %collective-permute-done.7.pair), channel_id=1, source_target_pairs={{0,1},{1,0},{2,3},{3,2},{4,5},{5,4},{6,7},{7,6},{8,9},{9,8},{10,11... | collective-permute-start | bytes 786440 | tf_op jit(solution)/shard_map/ppermute | solution.py:277
  133.6 1.5 %copy-start.8 = (f32[128,512]{1,0:T(8,128)}, f32[128,512]{1,0:T(8,128)S(1)}, u32[]{:S(2)}) copy-start(f32[128,512]{1,0:T(8,128)S(1)} %collective-permute-done.6.mate) | copy-start | bytes 786436
  135.1 0.7 copy-start.9

commit v2 on v1

--- a/solution.py
+++ b/solution.py
@@ -10,6 +10,7 @@
 LANES = 128
 SUB = 8
 GROUP = 4
+PANEL = 32
 VMEM_LIMIT = 60 * 1024 * 1024
 
 
@@ -29,6 +30,16 @@
     )
 
 
+def dot_nn(a, b):
+    a_high, a_low = split(a)
+    b_high, b_low = split(b)
+
+    def one(x, y):
+        return jnp.dot(x, y, preferred_element_type=jnp.float32)
+
+    return one(a_high, b_high) + (one(a_high, b_low) + one(a_low, b_high))
+
+
 def spread_lane(x, lane):
     return jnp.take_along_axis(x, jnp.full((SUB, LANES), lane, jnp.int32), 1, mode="promise_in_bounds")
 
@@ -37,7 +48,7 @@
     return jnp.take_along_axis(x, jnp.full((SUB, LANES), row, jnp.int32), 0, mode="promise_in_bounds")
 
 
-def eliminate_group(tiles, start, lane_ids, row_ids):
+def eliminate_group(tiles, start, stop, lane_ids, row_ids):
     tile, first = divmod(start, SUB)
     size = GROUP
     rows = [spread_row(tiles[tile], first + k) for k in range(size)]
@@ -67,7 +78,7 @@
         for m in range(k + 1, size):
             solved[k] = solved[k] - ratio[m, k] * solved[m]
     result = list(tiles)
-    for t in range(tile, len(tiles)):
+    for t in range(tile, stop):
         old = tiles[t]
         if t == tile and first + size == SUB:
             new = old
@@ -85,13 +96,32 @@
     return result
 
 
+def eliminate_below(tiles, low, stop):
+    done = jnp.concatenate(tiles[low:stop], axis=0)
+    below = jnp.concatenate(tiles[stop:], axis=0)
+    lanes = lax.broadcasted_iota(jnp.int32, done.shape, 1)
+    rows = lax.broadcasted_iota(jnp.int32, done.shape, 0)
+    done = jnp.where((lanes > low * SUB + rows) & (lanes < stop * SUB), 0.0, done)
+    lanes = lax.broadcasted_iota(jnp.int32, below.shape, 1)
+    inside = (lanes >= low * SUB) & (lanes < stop * SUB)
+    factors = dot_nt(jnp.where(inside, below, 0.0), done)
+    below = jnp.where(inside, 0.0, below) - dot_nn(factors, done)
+    count = len(tiles) - stop
+    return tiles[:stop] + [below[t * SUB : (t + 1) * SUB, :] for t in range(count)]
+
+
 def factor_inverses(blocks):
     lane_ids = lax.broadcasted_iota(jnp.int32, (SUB, LANES), 1)
     row_ids = lax.broadcasted_iota(jnp.int32, (SUB, LANES), 0)
     count = LANES // SUB
     tiles = [[b[t * SUB : (t + 1) * SUB, :] for t in range(count)] for b in blocks]
-    for start in range(0, LANES, GROUP):
-        tiles = [eliminate_group(t, start, lane_ids, row_ids) for t in tiles]
+    panel = LANES if len(blocks) == 1 else PANEL
+    for base in range(0, LANES, panel):
+        low, stop = base // SUB, (base + panel) // SUB
+        for start in range(base, base + panel, GROUP):
+            tiles = [eliminate_group(t, start, stop, lane_ids, row_ids) for t in tiles]
+        if stop < count:
+            tiles = [eliminate_below(t, low, stop) for t in tiles]
     rows = lax.broadcasted_iota(jnp.int32, (LANES, LANES), 0)
     columns = lax.broadcasted_iota(jnp.int32, (LANES, LANES), 1)
     return [jnp.where(columns <= rows, jnp.concatenate(t, axis=0), 0.0) for t in tiles]

time: 138 us -> 133 us (0.964); the launches traced: 138 us -> 131 us
  Pallas kernels: 79.1 us -> 75.7 us
  starting transfers between devices: 9.56 us -> 6.58 us
    ppermute x3, starting transfers between devices: 8.42 us -> 4.19 us  [pair(): return lax.ppermute(x, 'leaf', other_chip)]
    pallas_call x4, Pallas kernels: 79.1 us -> 75.7 us  [call(): pl.pallas_call(kernel, out_shape=made if many else made[0], in_specs=[sme...]
  transfers between devices with their start and end apart: 9 -> 9, of which waited for: 5 -> 5; matrix products, arithmetic and copies ran while one was open for 6% -> 6% of each run, Pallas kernels for 32% -> 30%
where the time goes in v2:
time: 133 us; the launch traced here: 131 us
  Pallas kernels  75.7 us (57%)
  waiting for transfers between devices  32.3 us (24%)
  local copies, waits for them, and re-layouts  13.6 us (10%)
  starting transfers between devices  6.58 us (5%)
  other arithmetic  1.77 us (1%)
  between operations  1.37 us (1%)
    pallas_call x4, Pallas kernels, call(): pl.pallas_call(kernel, out_shape=made if many else made[0], in_specs=[sme...  75.7 us
    ppermute x3, waiting for transfers between devices, pair(): return lax.ppermute(x, 'leaf', other_chip)  27.8 us
    ppermute x6, waiting for transfers between devices, mate(): return lax.ppermute(x, 'front', other_core)  4.56 us
    ppermute x3, starting transfers between devices, pair(): return lax.ppermute(x, 'leaf', other_chip)  4.19 us
    slice x1, local copies, waits for them, and re-layouts, on_device(): own_panel = child_fronts[:, :, :, :pivots]  4.15 us
    squeeze x1, local copies, waits for them, and re-layouts, on_device(): own22 = child_fronts[:, 1, :, pivots:]  3.52 us
  transfers between devices with their start and end apart: 9, of which 5 were waited for; matrix products, arithmetic and copies ran while one was open for 6% of the time, Pallas kernels for 30%

profile of v2, /device:TPU:0, one launch (start us, length us, event | category | flops | bytes accessed | tf_op | source)
XLA Modules:
  0.0 131.4 jit_solution(16538591854234966549)
XLA Ops:
  0.6 3.5 %slice_bitcast_fusion.1 = (f32[3,256,512]{2,1,0:T(8,128)S(1)}, f32[3,256,512]{2,1,0:T(8,128)}) fusion(f32[3,2,256,1024]{3,2,1,0:T(8,128)} %param.4), kind=kLoop, calls=%fused_computation.1 | loop fusion | bytes 6291456 | tf_op jit(solution)/shard_map/squeeze | solution.py:313
  4.1 0.0 copy-start.1
  4.2 0.5 collective-permute-start
  4.6 0.0 collective-permute-start.1
  4.7 4.1 %slice.21.own = f32[3,2,256,512]{3,2,1,0:T(8,128)} slice(f32[3,2,256,1024]{3,2,1,0:T(8,128)} %param.4), slice={[0:3], [0:2], [0:256], [0:512]} | slice | bytes 6291456 | tf_op jit(solution)/shard_map/slice | solution.py:312
  8.8 0.0 copy-done.1
  9.5 0.6 pad_add_fusion.place
  10.1 0.0 collective-permute-done.other
  10.1 39.4 %shard_map.67 = f32[3,2,256,512]{3,2,1,0:T(8,128)} custom-call(s32[3]{0:T(128)} %pad_add_fusion.place, f32[3,2,256,512]{3,2,1,0:T(8,128)} %slice.21.own, f32[3,256,512]{2,1,0:T(8,128)} %collective-permute-done.other), custom_call_target="tpu_custom_call" | custom-call | tf_op jit(solution)/shard_map/pallas_call | solution.py:287
  49.4 1.5 %slice_bitcast_fusion.own21 = f32[3,256,512]{2,1,0:T(8,128)S(1)} fusion(f32[3,2,256,512]{3,2,1,0:T(8,128)} %shard_map.67), kind=kLoop, calls=%fused_computation | loop fusion | bytes 3145728 | tf_op jit(solution)/shard_map/squeeze | solution.py:324
  51.0 0.0 copy-start
  51.0 0.6 collective-permute-start.2
  51.5 0.0 collective-permute-done.1.other22
  51.5 3.0 %collective-permute-done.2.other21 = f32[3,256,512]{2,1,0:T(8,128)S(1)} collective-permute-done((f32[3,256,512]{2,1,0:T(8,128)S(1)}, f32[3,256,512]{2,1,0:T(8,128)S(1)}, u32[]{:S(2)}, u32[]{:S(2)}) %collective-permute-start.2) | collective-permute-done | bytes 1572896 | tf_op jit(solution)/shard_map/ppermute | solution.py:307
  54.6 0.0 copy-start.3
  54.6 1.1 copy-done.3
  55.7 0.0 copy-done
  55.7 7.1 %shard_map.68 = (f32[2,128,512]{2,1,0:T(8,128)}, f32[128,1024]{1,0:T(8,128)}, f32[128,1024]{1,0:T(8,128)}) custom-call(s32[3]{0:T(128)} %pad_add_fusion.place, s32[3,4]{1,0:T(4,128)} %maps.1, f32[3,256,512]{2,1,0:T(8,128)} %copy-done.1, f32[3,256,512]{2,1,0:T(8,128)} %collective-permute-done.1.other22, f32[3,256,512]{2,1,0:T(8,128)} %copy-done, ...), custom_call_target="tpu_custom_call" | custom-call | tf_op jit(solution)/shard_map/pallas_call | solution.py:287
  62.8 0.0 copy-start.5
  62.8 2.1 %collective-permute-start.3 = (f32[2,128,512]{2,1,0:T(8,128)}, f32[2,128,512]{2,1,0:T(8,128)S(1)}, u32[]{:S(2)}, u32[]{:S(2)}) collective-permute-start(f32[2,128,512]{2,1,0:T(8,128)} %get-tuple-element.6), channel_id=1, source_target_pairs={{0,2},{2,0},{4,6},{6,4},{8,10},{10,8},{12,14},{14,12},{16,18},{18,... | collective-permute-start | bytes 1572872 | tf_op jit(solution)/shard_map/ppermute | solution.py:310
  64.9 0.1 collective-permute-start.5
  65.0 12.6 %collective-permute-done.3 = f32[2,128,512]{2,1,0:T(8,128)S(1)} collective-permute-done((f32[2,128,512]{2,1,0:T(8,128)}, f32[2,128,512]{2,1,0:T(8,128)S(1)}, u32[]{:S(2)}, u32[]{:S(2)}) %collective-permute-start.3) | collective-permute-done | bytes 524320 | tf_op jit(solution)/shard_map/ppermute | solution.py:310
  77.5 1.1 add.11.mine
  78.6 0.0 copy-start.2
  78.7 1.3 %collective-permute-start.4 = (f32[2,128,512]{2,1,0:T(8,128)S(1)}, f32[2,128,512]{2,1,0:T(8,128)S(1)}, u32[]{:S(2)}, u32[]{:S(2)}) collective-permute-start(f32[2,128,512]{2,1,0:T(8,128)S(1)} %add.11.mine), channel_id=1, source_target_pairs={{0,1},{1,0},{2,3},{3,2},{4,5},{5,4},{6,7},{7,6},{8,9},{9,8},{10,11... | collective-permute-start | bytes 1572872 | tf_op jit(solution)/shard_map/ppermute | solution.py:307
  80.0 8.4 %collective-permute-done.5 = f32[128,1024]{1,0:T(8,128)S(1)} collective-permute-done((f32[128,1024]{1,0:T(8,128)}, f32[128,1024]{1,0:T(8,128)S(1)}, u32[]{:S(2)}, u32[]{:S(2)}) %collective-permute-start.5) | collective-permute-done | bytes 524320 | tf_op jit(solution)/shard_map/ppermute | solution.py:310
  88.3 0.0 copy-done.5
  88.3 0.1 add.12
  88.4 0.8 fusion
  89.2 0.0 collective-permute-done.4.yours
  89.2 0.0 copy-start.6
  89.2 0.0 copy-done.2
  89.2 0.8 copy-done.6
  90.0 26.7 %shard_map.69 = f32[2,128,512]{2,1,0:T(8,128)} custom-call(s32[3]{0:T(128)} %pad_add_fusion.place, f32[2,128,512]{2,1,0:T(8,128)} %copy-done.2, f32[2,128,512]{2,1,0:T(8,128)} %copy-done.6, f32[128,512]{1,0:T(8,128)} %get-tuple-element.12.lower), custom_call_target="tpu_custom_call" | custom-call | tf_op jit(solution)/shard_map/pallas_call | solution.py:287
  116.7 1.0 slice_bitcast_fusion.3.own
  117.7 0.0 copy-start.4
  117.7 2.0 %collective-permute-start.7 = (f32[128,512]{1,0:T(8,128)S(1)}, f32[128,512]{1,0:T(8,128)S(1)}, u32[]{:S(2)}, u32[]{:S(2)}) collective-permute-start(f32[128,512]{1,0:T(8,128)S(1)} %slice_bitcast_fusion.3.own), channel_id=1, source_target_pairs={{0,2},{2,0},{4,6},{6,4},{8,10},{10,8},{12,14},{14,12},{16,18},{18,... | collective-permute-start | bytes 786440 | tf_op jit(solution)/shard_map/ppermute | solution.py:310
  119.7 0.0 collective-permute-start.6
  119.7 6.9 %collective-permute-done.7.pair = f32[128,512]{1,0:T(8,128)S(1)} collective-permute-done((f32[128,512]{1,0:T(8,128)S(1)}, f32[128,512]{1,0:T(8,128)S(1)}, u32[]{:S(2)}, u32[]{:S(2)}) %collective-permute-start.7) | collective-permute-done | bytes 262176 | tf_op jit(solution)/shard_map/ppermute | solution.py:310
  126.6 0.0 collective-permute-start.8
  126.6 0.0 collective-permute-done.6.mate
  126.6 0.0 copy-start.8
  126.6 1.5 %collective-permute-done.8.cross = f32[128,512]{1,0:T(8,128)S(1)} collective-permute-done((f32[128,512]{1,0:T(8,128)S(1)}, f32[128,512]{1,0:T(8,128)S(1)}, u32[]{:S(2)}, u32[]{:S(2)}) %collective-permute-start.8) | collective-permute-done | bytes 262176 | tf_op jit(solution)/shard_map/ppermute | solution.py:307
  128.1 0.0 copy-done.4
  128.1 0.0 copy-done.7
  128.1 0.0 copy-done.8
  128.1 0.7 copy-done.9
  128.8 2.6 %shard_map.70 = f32[128,512]{1,0:T(8,128)} custom-call(s32[3]{0:T(128)} %pad_add_fusion.place, f32[128,512]{1,0:T(8,128)} %get-tuple-element.11.base, f32[128,512]{1,0:T(8,128)} %copy-done.4, f32[128,512]{1,0:T(8,128)} %copy-done.8, f32[128,512]{1,0:T(8,128)} %copy-done.7, f32[128,512]{1,0:T(8,128)} %copy-done.9), custom_call_target="tpu_custom_call" | custom-call | tf_op jit(solution)/shard_map/pallas_call | solution.py:287
  (2 shorter events, 0.0 us)
Async XLA Ops:
  4.1 4.7 %copy-start.1 = (f32[3,256,512]{2,1,0:T(8,128)}, f32[3,256,512]{2,1,0:T(8,128)S(1)}, u32[]{:S(2)}) copy-start(f32[3,256,512]{2,1,0:T(8,128)S(1)} %get-tuple-element.9.own22) | copy-start | bytes 4718596
  4.2 5.9 %collective-permute-start = (f32[3,256,512]{2,1,0:T(8,128)}, f32[3,256,512]{2,1,0:T(8,128)}, u32[]{:S(2)}, u32[]{:S(2)}) collective-permute-start(f32[3,256,512]{2,1,0:T(8,128)} %get-tuple-element.10), channel_id=1, source_target_pairs={{0,1},{1,0},{2,3},{3,2},{4,5},{5,4},{6,7},{7,6},{8,9},{9,8},{10,11... | collective-permute-start | bytes 4718600 | tf_op jit(solution)/shard_map/ppermute | solution.py:307
  4.6 46.9 %collective-permute-start.1 = (f32[3,256,512]{2,1,0:T(8,128)S(1)}, f32[3,256,512]{2,1,0:T(8,128)}, u32[]{:S(2)}, u32[]{:S(2)}) collective-permute-start(f32[3,256,512]{2,1,0:T(8,128)S(1)} %get-tuple-element.9.own22), channel_id=1, source_target_pairs={{0,1},{1,0},{2,3},{3,2},{4,5},{5,4},{6,7},{7,6},{8,9},{9,8},{10,11... | collective-permute-start | bytes 4718600 | tf_op jit(solution)/shard_map/ppermute | solution.py:307
  51.0 4.7 %copy-start = (f32[3,256,512]{2,1,0:T(8,128)}, f32[3,256,512]{2,1,0:T(8,128)S(1)}, u32[]{:S(2)}) copy-start(f32[3,256,512]{2,1,0:T(8,128)S(1)} %slice_bitcast_fusion.own21) | copy-start | bytes 4718596
  51.0 3.6 %collective-permute-start.2 = (f32[3,256,512]{2,1,0:T(8,128)S(1)}, f32[3,256,512]{2,1,0:T(8,128)S(1)}, u32[]{:S(2)}, u32[]{:S(2)}) collective-permute-start(f32[3,256,512]{2,1,0:T(8,128)S(1)} %slice_bitcast_fusion.own21), channel_id=1, source_target_pairs={{0,1},{1,0},{2,3},{3,2},{4,5},{5,4},{6,7},{7,6},{8,9},{9,8},{10,11... | collective-permute-start | bytes 4718600 | tf_op jit(solution)/shard_map/ppermute | solution.py:307
  54.6 1.1 copy-start.3
  62.8 25.5 %copy-start.5 = (f32[128,1024]{1,0:T(8,128)S(1)}, f32[128,1024]{1,0:T(8,128)}, u32[]{:S(2)}) copy-start(f32[128,1024]{1,0:T(8,128)} %get-tuple-element.7) | copy-start | bytes 1572868
  62.8 14.7 %collective-permute-start.3 = (f32[2,128,512]{2,1,0:T(8,128)}, f32[2,128,512]{2,1,0:T(8,128)S(1)}, u32[]{:S(2)}, u32[]{:S(2)}) collective-permute-start(f32[2,128,512]{2,1,0:T(8,128)} %get-tuple-element.6), channel_id=1, source_target_pairs={{0,2},{2,0},{4,6},{6,4},{8,10},{10,8},{12,14},{14,12},{16,18},{18,... | collective-permute-start | bytes 1572872 | tf_op jit(solution)/shard_map/ppermute | solution.py:310
  64.9 23.4 %collective-permute-start.5 = (f32[128,1024]{1,0:T(8,128)}, f32[128,1024]{1,0:T(8,128)S(1)}, u32[]{:S(2)}, u32[]{:S(2)}) collective-permute-start(f32[128,1024]{1,0:T(8,128)} %get-tuple-element.8), channel_id=1, source_target_pairs={{0,2},{2,0},{4,6},{6,4},{8,10},{10,8},{12,14},{14,12},{16,18},{18,... | collective-permute-start | bytes 1572872 | tf_op jit(solution)/shard_map/ppermute | solution.py:310
  78.6 10.6 %copy-start.2 = (f32[2,128,512]{2,1,0:T(8,128)}, f32[2,128,512]{2,1,0:T(8,128)S(1)}, u32[]{:S(2)}) copy-start(f32[2,128,512]{2,1,0:T(8,128)S(1)} %add.11.mine) | copy-start | bytes 1572868
  78.7 10.6 %collective-permute-start.4 = (f32[2,128,512]{2,1,0:T(8,128)S(1)}, f32[2,128,512]{2,1,0:T(8,128)S(1)}, u32[]{:S(2)}, u32[]{:S(2)}) collective-permute-start(f32[2,128,512]{2,1,0:T(8,128)S(1)} %add.11.mine), channel_id=1, source_target_pairs={{0,1},{1,0},{2,3},{3,2},{4,5},{5,4},{6,7},{7,6},{8,9},{9,8},{10,11... | collective-permute-start | bytes 1572872 | tf_op jit(solution)/shard_map/ppermute | solution.py:307
  89.2 0.8 copy-start.6
  117.7 10.4 %copy-start.4 = (f32[128,512]{1,0:T(8,128)}, f32[128,512]{1,0:T(8,128)S(1)}, u32[]{:S(2)}) copy-start(f32[128,512]{1,0:T(8,128)S(1)} %slice_bitcast_fusion.3.own) | copy-start | bytes 786436
  117.7 8.9 %collective-permute-start.7 = (f32[128,512]{1,0:T(8,128)S(1)}, f32[128,512]{1,0:T(8,128)S(1)}, u32[]{:S(2)}, u32[]{:S(2)}) collective-permute-start(f32[128,512]{1,0:T(8,128)S(1)} %slice_bitcast_fusion.3.own), channel_id=1, source_target_pairs={{0,2},{2,0},{4,6},{6,4},{8,10},{10,8},{12,14},{14,12},{16,18},{18,... | collective-permute-start | bytes 786440 | tf_op jit(solution)/shard_map/ppermute | solution.py:310
  119.7 6.9 %collective-permute-start.6 = (f32[128,512]{1,0:T(8,128)S(1)}, f32[128,512]{1,0:T(8,128)S(1)}, u32[]{:S(2)}, u32[]{:S(2)}) collective-permute-start(f32[128,512]{1,0:T(8,128)S(1)} %slice_bitcast_fusion.3.own), channel_id=1, source_target_pairs={{0,1},{1,0},{2,3},{3,2},{4,5},{5,4},{6,7},{7,6},{8,9},{9,8},{10,11... | collective-permute-start | bytes 786440 | tf_op jit(solution)/shard_map/ppermute | solution.py:307
  126.6 1.5 %copy-start.7 = (f32[128,512]{1,0:T(8,128)}, f32[128,512]{1,0:T(8,128)S(1)}, u32[]{:S(2)}) copy-start(f32[128,512]{1,0:T(8,128)S(1)} %collective-permute-done.7.pair) | copy-start | bytes 786436
  126.6 1.5 %collective-permute-start.8 = (f32[128,512]{1,0:T(8,128)S(1)}, f32[128,512]{1,0:T(8,128)S(1)}, u32[]{:S(2)}, u32[]{:S(2)}) collective-permute-start(f32[128,512]{1,0:T(8,128)S(1)} %collective-permute-done.7.pair), channel_id=1, source_target_pairs={{0,1},{1,0},{2,3},{3,2},{4,5},{5,4},{6,7},{7,6},{8,9},{9,8},{10,11... | collective-permute-start | bytes 786440 | tf_op jit(solution)/shard_map/ppermute | solution.py:307
  126.6 1.5 %copy-start.8 = (f32[128,512]{1,0:T(8,128)}, f32[128,512]{1,0:T(8,128)S(1)}, u32[]{:S(2)}) copy-start(f32[128,512]{1,0:T(8,128)S(1)} %collective-permute-done.6.mate) | copy-start | bytes 786436
  128.1 0.7 copy-start.9

commit v3 on v2

--- a/solution.py
+++ b/solution.py
@@ -217,8 +217,18 @@
     pivot_out[...] = jnp.zeros_like(pivot_out)
     keep_out[...] = parent[1]
     send_out[...] = jnp.zeros_like(send_out)
-    pivot_out[half] = parent[0, :, : pivot_out.shape[2]]
-    pivot_blocks = pivot_out.shape[2] // block
+    pivots = parent.shape[2] // 2
+    first = pivots // 2
+    pivot_blocks = pivots // block
+
+    @pl.when(half == 0)
+    def _():
+        pivot_out[:, :first] = parent[0, :, :first]
+
+    @pl.when(half == 1)
+    def _():
+        pivot_out[:, first:] = parent[0, :, :pivots]
+
 
     @pl.loop(0, slots)
     def _(s):
@@ -239,9 +249,11 @@
                     column = maps[s, b]
                     there = pl.ds(pl.multiple_of(column * block, block), block)
 
-                    @pl.when((target < pivot_blocks) & (column < pivot_blocks))
+                    packed = pl.ds(pl.multiple_of(owner * first + column * block, block), block)
+
+                    @pl.when((target < pivot_blocks) & (column <= target))
                     def _():
-                        pivot_out[owner, :, there] += tile
+                        pivot_out[:, packed] += tile
 
                     @pl.when((target >= pivot_blocks) & (owner == half))
                     def _():
@@ -252,17 +264,26 @@
                         send_out[:, there] += tile
 
 
-def parent_kernel(place, mine, yours, lower, out, work, saved):
+def parent_kernel(place, mine, yours, out, work, saved):
     core, half = place[0], place[2]
-    _, rows, pivots = mine.shape
-    for h in range(2):
-        work[0, pl.ds(pl.multiple_of((2 * h + core) * rows, rows), rows), :] = mine[h]
-        work[0, pl.ds(pl.multiple_of((2 * h + 1 - core) * rows, rows), rows), :] = yours[h]
-    out[1] = lower[...]
+    rows = mine.shape[0]
+    pivots = out.shape[1]
+    first = pivots // 2
+    for source, side in ((mine, core), (yours, 1 - core)):
+        low = pl.ds(pl.multiple_of(side * rows, rows), rows)
+        high = pl.ds(pl.multiple_of((2 + side) * rows, rows), rows)
+        work[0, low, :first] = source[:, :first]
+        work[0, high, :] = source[:, first:]
     factor_pivots(work, saved)
     clear_upper(work, pivots)
-    solve_rows(work, saved, [out.at[1]])
-    out[0] = work[0, pl.ds(pl.multiple_of((2 * half + core) * rows, rows), rows), :]
+    out[...] = work[0, pl.ds(pl.multiple_of((2 * half + core) * rows, rows), rows), :]
+
+
+def lower_kernel(work, saved, keep, received, out, rest):
+    pivots = out.shape[1]
+    out[...] = keep[:, :pivots] + received[:, :pivots]
+    rest[...] = keep[:, pivots:] + received[:, pivots:]
+    solve_rows(work, saved, [out])
 
 
 def update_kernel(place, base, own, mate, pair, cross, out):
@@ -327,7 +348,7 @@
     parent_pivots = parent_order // 2
     pivot_part, keep, send = call(
         add_kernel,
-        [(2, rows, parent_pivots), (rows, parent_order), (rows, parent_order)],
+        [(rows, parent_pivots + parent_pivots // 2), (rows, parent_order), (rows, parent_order)],
         [(slots, order - pivots, pivots)],
         [place, row_map],
         own22,
@@ -336,26 +357,37 @@
         other21,
         parent_fronts[0],
     )
-    pivot_mine = pivot_part + pair(pivot_part)
+    pivot_received, send = lax.optimization_barrier((pair(pivot_part), send))
+    pivot_mine = pivot_part + pivot_received
     pivot_yours = mate(pivot_mine)
-    lower = keep + pair(send)
-    panel = call(
+    received = pair(send)
+    steps = parent_pivots // LANES
+    factor, work, saved = call(
         parent_kernel,
-        (2, rows, parent_pivots),
-        [(1, parent_pivots, parent_pivots), (1, parent_pivots // LANES, LANES, LANES)],
+        [(rows, parent_pivots), (1, parent_pivots, parent_pivots), (1, steps, LANES, LANES)],
+        [],
         [place],
         pivot_mine,
         pivot_yours,
-        lower[:, :parent_pivots],
-    )
-    lower21 = panel[1]
+    )
+    lower21, rest = call(
+        lower_kernel,
+        [(rows, parent_pivots), (rows, parent_order - parent_pivots)],
+        [],
+        [],
+        work,
+        saved,
+        keep,
+        received,
+    )
+    panel = jnp.stack([factor, lower21])
     from_pair = pair(lower21)
     update = call(
         update_kernel,
         (rows, parent_order - parent_pivots),
         [],
         [place],
-        lower[:, parent_pivots:],
+        rest,
         lower21,
         mate(lower21),
         from_pair,

time: 133 us -> 126 us (0.947)
  waiting for transfers between devices: 32.3 us -> 22.7 us
  Pallas kernels: 75.7 us -> 77.6 us
  other arithmetic: 1.77 us -> 3.48 us
    ppermute x3, waiting for transfers between devices: 27.8 us -> 17.9 us  [pair(): return lax.ppermute(x, 'leaf', other_chip)]
    pallas_call x4 -> x5, Pallas kernels: 75.7 us -> 77.6 us  [call(): pl.pallas_call(kernel, out_shape=made if many else made[0], in_specs=[sme...]
    broadcast_in_dim x0 -> x1, other arithmetic: none -> 1.87 us  [on_device(): return (child_panels, panel[None], update[None])]
  transfers between devices with their start and end apart: 9 -> 9, of which waited for: 5 -> 4; matrix products, arithmetic and copies ran while one was open for 6% -> 7% of each run, Pallas kernels for 30% -> 53%
where the time goes in v3:
time: 126 us; the launch traced here: 124 us
  Pallas kernels  77.6 us (62%)
  waiting for transfers between devices  22.7 us (18%)
  local copies, waits for them, and re-layouts  12.7 us (10%)
  starting transfers between devices  5.98 us (5%)
  other arithmetic  3.48 us (3%)
  between operations  1.37 us (1%)
    pallas_call x5, Pallas kernels, call(): pl.pallas_call(kernel, out_shape=made if many else made[0], in_specs=[sme...  77.6 us
    ppermute x3, waiting for transfers between devices, pair(): return lax.ppermute(x, 'leaf', other_chip)  17.9 us
    ppermute x3, starting transfers between devices, pair(): return lax.ppermute(x, 'leaf', other_chip)  4.84 us
    ppermute x6, waiting for transfers between devices, mate(): return lax.ppermute(x, 'front', other_core)  4.75 us
    slice x1, local copies, waits for them, and re-layouts, on_device(): own_panel = child_fronts[:, :, :, :pivots]  4.14 us
    squeeze x1, local copies, waits for them, and re-layouts, on_device(): own22 = child_fronts[:, 1, :, pivots:]  3.63 us
    unnamed x20, local copies, waits for them, and re-layouts  3.45 us
  transfers between devices with their start and end apart: 9, of which 4 were waited for; matrix products, arithmetic and copies ran while one was open for 7% of the time, Pallas kernels for 53%

profile of v3, /device:TPU:0, one launch (start us, length us, event | category | flops | bytes accessed | tf_op | source)
XLA Modules:
  0.0 123.9 jit_solution(4701497973931025918)
XLA Ops:
  0.6 3.6 %slice_bitcast_fusion.1 = (f32[3,256,512]{2,1,0:T(8,128)S(1)}, f32[3,256,512]{2,1,0:T(8,128)}) fusion(f32[3,2,256,1024]{3,2,1,0:T(8,128)} %param.4), kind=kLoop, calls=%fused_computation.1 | loop fusion | bytes 6291456 | tf_op jit(solution)/shard_map/squeeze | solution.py:334
  4.3 0.0 copy-start.1
  4.3 0.5 collective-permute-start
  4.8 0.0 collective-permute-start.1
  4.8 4.1 %slice.12.own = f32[3,2,256,512]{3,2,1,0:T(8,128)} slice(f32[3,2,256,1024]{3,2,1,0:T(8,128)} %param.4), slice={[0:3], [0:2], [0:256], [0:512]} | slice | bytes 6291456 | tf_op jit(solution)/shard_map/slice | solution.py:333
  8.9 0.0 copy-done.1
  9.6 0.6 pad_add_fusion.place
  10.1 0.0 collective-permute-done.other
  10.1 39.4 %shard_map.67 = f32[3,2,256,512]{3,2,1,0:T(8,128)} custom-call(s32[3]{0:T(128)} %pad_add_fusion.place, f32[3,2,256,512]{3,2,1,0:T(8,128)} %slice.12.own, f32[3,256,512]{2,1,0:T(8,128)} %collective-permute-done.other), custom_call_target="tpu_custom_call" | custom-call | tf_op jit(solution)/shard_map/pallas_call | solution.py:308
  49.5 1.5 %slice_bitcast_fusion.own21 = f32[3,256,512]{2,1,0:T(8,128)S(1)} fusion(f32[3,2,256,512]{3,2,1,0:T(8,128)} %shard_map.67), kind=kLoop, calls=%fused_computation | loop fusion | bytes 3145728 | tf_op jit(solution)/shard_map/squeeze | solution.py:345
  51.0 0.0 copy-start
  51.1 0.6 collective-permute-start.2
  51.6 0.0 collective-permute-done.1.other22
  51.6 3.0 %collective-permute-done.2.other21 = f32[3,256,512]{2,1,0:T(8,128)S(1)} collective-permute-done((f32[3,256,512]{2,1,0:T(8,128)S(1)}, f32[3,256,512]{2,1,0:T(8,128)S(1)}, u32[]{:S(2)}, u32[]{:S(2)}) %collective-permute-start.2) | collective-permute-done | bytes 1572896 | tf_op jit(solution)/shard_map/ppermute | solution.py:328
  54.7 0.0 copy-start.2
  54.7 1.1 copy-done.2
  55.8 0.0 copy-done
  55.8 6.4 %shard_map.68 = (f32[128,768]{1,0:T(8,128)}, f32[128,1024]{1,0:T(8,128)}, f32[128,1024]{1,0:T(8,128)}) custom-call(s32[3]{0:T(128)} %pad_add_fusion.place, s32[3,4]{1,0:T(4,128)} %maps.1, f32[3,256,512]{2,1,0:T(8,128)} %copy-done.1, f32[3,256,512]{2,1,0:T(8,128)} %collective-permute-done.1.other22, f32[3,256,512]{2,1,0:T(8,128)} %copy-done, ...), custom_call_target="tpu_custom_call" | custom-call | tf_op jit(solution)/shard_map/pallas_call | solution.py:308
  62.2 2.8 %collective-permute-start.3 = (f32[128,768]{1,0:T(8,128)}, f32[128,768]{1,0:T(8,128)S(1)}, u32[]{:S(2)}, u32[]{:S(2)}) collective-permute-start(f32[128,768]{1,0:T(8,128)} %get-tuple-element.13), channel_id=1, source_target_pairs={{0,2},{2,0},{4,6},{6,4},{8,10},{10,8},{12,14},{14,12},{16,18},{18,... | collective-permute-start | bytes 1179656 | tf_op jit(solution)/shard_map/ppermute | solution.py:331
  65.0 9.6 %collective-permute-done.3 = f32[128,768]{1,0:T(8,128)S(1)} collective-permute-done((f32[128,768]{1,0:T(8,128)}, f32[128,768]{1,0:T(8,128)S(1)}, u32[]{:S(2)}, u32[]{:S(2)}) %collective-permute-start.3) | collective-permute-done | bytes 393248 | tf_op jit(solution)/shard_map/ppermute | solution.py:331
  74.7 1.7 %collective-permute-start.5 = (f32[128,1024]{1,0:T(8,128)}, f32[128,1024]{1,0:T(8,128)S(1)}, u32[]{:S(2)}, u32[]{:S(2)}) collective-permute-start(f32[128,1024]{1,0:T(8,128)} %get-tuple-element.20), channel_id=1, source_target_pairs={{0,2},{2,0},{4,6},{6,4},{8,10},{10,8},{12,14},{14,12},{16,18},{18,... | collective-permute-start | bytes 1572872 | tf_op jit(solution)/shard_map/ppermute | solution.py:331
  76.4 1.0 add.8.mine
  77.5 0.0 copy-start.3
  77.5 0.1 collective-permute-start.4
  77.6 1.7 %collective-permute-done.4.yours = f32[128,768]{1,0:T(8,128)S(1)} collective-permute-done((f32[128,768]{1,0:T(8,128)S(1)}, f32[128,768]{1,0:T(8,128)S(1)}, u32[]{:S(2)}, u32[]{:S(2)}) %collective-permute-start.4) | collective-permute-done | bytes 393248 | tf_op jit(solution)/shard_map/ppermute | solution.py:328
  79.3 0.0 copy-done.3
  79.3 0.0 copy-start.5
  79.3 0.7 copy-done.5
  80.0 25.8 %shard_map.69 = (f32[128,512]{1,0:T(8,128)}, f32[1,512,512]{2,1,0:T(8,128)}, f32[1,4,128,128]{3,2,1,0:T(8,128)}) custom-call(s32[3]{0:T(128)} %pad_add_fusion.place, f32[128,768]{1,0:T(8,128)} %copy-done.3, f32[128,768]{1,0:T(8,128)} %copy-done.5), custom_call_target="tpu_custom_call" | custom-call | tf_op jit(solution)/shard_map/pallas_call | solution.py:308
  105.8 0.0 copy-start.6
  105.8 0.0 collective-permute-done.5.received
  105.8 0.0 copy-start.4
  105.8 0.8 copy-done.4
  106.6 3.5 %shard_map.70 = (f32[128,512]{1,0:T(8,128)}, f32[128,512]{1,0:T(8,128)}) custom-call(f32[1,512,512]{2,1,0:T(8,128)} %get-tuple-element.17.work, f32[1,4,128,128]{3,2,1,0:T(8,128)} %get-tuple-element.18.saved, f32[128,1024]{1,0:T(8,128)} %get-tuple-element.19.keep, f32[128,1024]{1,0:T(8,128)} %copy-done.4), custom_call_target="tpu_custom_call" | custom-call | tf_op jit(solution)/shard_map/pallas_call | solution.py:308
  110.1 0.3 collective-permute-start.7
  110.4 0.0 collective-permute-start.6
  110.4 8.3 %collective-permute-done.7.pair = f32[128,512]{1,0:T(8,128)S(1)} collective-permute-done((f32[128,512]{1,0:T(8,128)}, f32[128,512]{1,0:T(8,128)S(1)}, u32[]{:S(2)}, u32[]{:S(2)}) %collective-permute-start.7) | collective-permute-done | bytes 262176 | tf_op jit(solution)/shard_map/ppermute | solution.py:331
  118.6 0.0 copy-start.7
  118.6 0.0 collective-permute-start.8
  118.6 0.0 copy-done.6
  118.6 1.9 %maximum_bitcast_fusion = f32[1,2,128,512]{3,2,1,0:T(8,128)} fusion(f32[1,128,512]{2,1,0:T(8,128)} %bitcast.21, f32[1,128,512]{2,1,0:T(8,128)S(1)} %bitcast.22), kind=kLoop, calls=%fused_computation.3 | loop fusion | flops 131072 | bytes 1048576 | tf_op jit(solution)/shard_map/broadcast_in_dim | solution.py:396
  120.5 0.0 collective-permute-done.6.mate
  120.5 0.0 collective-permute-done.8.cross
  120.5 0.0 copy-start.9
  120.5 0.0 copy-done.7
  120.5 0.7 copy-done.8
  121.2 0.1 copy-done.9
  121.3 2.6 %shard_map.71 = f32[128,512]{1,0:T(8,128)} custom-call(s32[3]{0:T(128)} %pad_add_fusion.place, f32[128,512]{1,0:T(8,128)} %get-tuple-element.22.base, f32[128,512]{1,0:T(8,128)} %get-tuple-element.21.own, f32[128,512]{1,0:T(8,128)} %copy-done.8, f32[128,512]{1,0:T(8,128)} %copy-done.7, f32[128,512]{1,0:T(8,128)} %copy-done.9), custom_call_target="tpu_custom_call" | custom-call | tf_op jit(solution)/shard_map/pallas_call | solution.py:308
  (1 shorter events, 0.0 us)
Async XLA Ops:
  4.3 4.7 %copy-start.1 = (f32[3,256,512]{2,1,0:T(8,128)}, f32[3,256,512]{2,1,0:T(8,128)S(1)}, u32[]{:S(2)}) copy-start(f32[3,256,512]{2,1,0:T(8,128)S(1)} %get-tuple-element.23.own22) | copy-start | bytes 4718596
  4.3 5.9 %collective-permute-start = (f32[3,256,512]{2,1,0:T(8,128)}, f32[3,256,512]{2,1,0:T(8,128)}, u32[]{:S(2)}, u32[]{:S(2)}) collective-permute-start(f32[3,256,512]{2,1,0:T(8,128)} %get-tuple-element.24), channel_id=1, source_target_pairs={{0,1},{1,0},{2,3},{3,2},{4,5},{5,4},{6,7},{7,6},{8,9},{9,8},{10,11... | collective-permute-start | bytes 4718600 | tf_op jit(solution)/shard_map/ppermute | solution.py:328
  4.8 46.9 %collective-permute-start.1 = (f32[3,256,512]{2,1,0:T(8,128)S(1)}, f32[3,256,512]{2,1,0:T(8,128)}, u32[]{:S(2)}, u32[]{:S(2)}) collective-permute-start(f32[3,256,512]{2,1,0:T(8,128)S(1)} %get-tuple-element.23.own22), channel_id=1, source_target_pairs={{0,1},{1,0},{2,3},{3,2},{4,5},{5,4},{6,7},{7,6},{8,9},{9,8},{10,11... | collective-permute-start | bytes 4718600 | tf_op jit(solution)/shard_map/ppermute | solution.py:328
  51.0 4.7 %copy-start = (f32[3,256,512]{2,1,0:T(8,128)}, f32[3,256,512]{2,1,0:T(8,128)S(1)}, u32[]{:S(2)}) copy-start(f32[3,256,512]{2,1,0:T(8,128)S(1)} %slice_bitcast_fusion.own21) | copy-start | bytes 4718596
  51.1 3.6 %collective-permute-start.2 = (f32[3,256,512]{2,1,0:T(8,128)S(1)}, f32[3,256,512]{2,1,0:T(8,128)S(1)}, u32[]{:S(2)}, u32[]{:S(2)}) collective-permute-start(f32[3,256,512]{2,1,0:T(8,128)S(1)} %slice_bitcast_fusion.own21), channel_id=1, source_target_pairs={{0,1},{1,0},{2,3},{3,2},{4,5},{5,4},{6,7},{7,6},{8,9},{9,8},{10,11... | collective-permute-start | bytes 4718600 | tf_op jit(solution)/shard_map/ppermute | solution.py:328
  54.7 1.1 copy-start.2
  62.2 12.5 %collective-permute-start.3 = (f32[128,768]{1,0:T(8,128)}, f32[128,768]{1,0:T(8,128)S(1)}, u32[]{:S(2)}, u32[]{:S(2)}) collective-permute-start(f32[128,768]{1,0:T(8,128)} %get-tuple-element.13), channel_id=1, source_target_pairs={{0,2},{2,0},{4,6},{6,4},{8,10},{10,8},{12,14},{14,12},{16,18},{18,... | collective-permute-start | bytes 1179656 | tf_op jit(solution)/shard_map/ppermute | solution.py:331
  74.7 31.1 %collective-permute-start.5 = (f32[128,1024]{1,0:T(8,128)}, f32[128,1024]{1,0:T(8,128)S(1)}, u32[]{:S(2)}, u32[]{:S(2)}) collective-permute-start(f32[128,1024]{1,0:T(8,128)} %get-tuple-element.20), channel_id=1, source_target_pairs={{0,2},{2,0},{4,6},{6,4},{8,10},{10,8},{12,14},{14,12},{16,18},{18,... | collective-permute-start | bytes 1572872 | tf_op jit(solution)/shard_map/ppermute | solution.py:331
  77.5 1.8 %copy-start.3 = (f32[128,768]{1,0:T(8,128)}, f32[128,768]{1,0:T(8,128)S(1)}, u32[]{:S(2)}) copy-start(f32[128,768]{1,0:T(8,128)S(1)} %add.8.mine) | copy-start | bytes 1179652
  77.5 1.8 %collective-permute-start.4 = (f32[128,768]{1,0:T(8,128)S(1)}, f32[128,768]{1,0:T(8,128)S(1)}, u32[]{:S(2)}, u32[]{:S(2)}) collective-permute-start(f32[128,768]{1,0:T(8,128)S(1)} %add.8.mine), channel_id=1, source_target_pairs={{0,1},{1,0},{2,3},{3,2},{4,5},{5,4},{6,7},{7,6},{8,9},{9,8},{10,11... | collective-permute-start | bytes 1179656 | tf_op jit(solution)/shard_map/ppermute | solution.py:328
  79.3 0.7 copy-start.5
  105.8 12.8 %copy-start.6 = (f32[128,512]{1,0:T(8,128)S(1)}, f32[128,512]{1,0:T(8,128)}, u32[]{:S(2)}) copy-start(f32[128,512]{1,0:T(8,128)} %get-tuple-element.16) | copy-start | bytes 786436
  105.8 0.8 copy-start.4
  110.1 8.6 %collective-permute-start.7 = (f32[128,512]{1,0:T(8,128)}, f32[128,512]{1,0:T(8,128)S(1)}, u32[]{:S(2)}, u32[]{:S(2)}) collective-permute-start(f32[128,512]{1,0:T(8,128)} %get-tuple-element.21.own), channel_id=1, source_target_pairs={{0,2},{2,0},{4,6},{6,4},{8,10},{10,8},{12,14},{14,12},{16,18},{18,... | collective-permute-start | bytes 786440 | tf_op jit(solution)/shard_map/ppermute | solution.py:331
  110.4 10.2 %collective-permute-start.6 = (f32[128,512]{1,0:T(8,128)}, f32[128,512]{1,0:T(8,128)S(1)}, u32[]{:S(2)}, u32[]{:S(2)}) collective-permute-start(f32[128,512]{1,0:T(8,128)} %get-tuple-element.21.own), channel_id=1, source_target_pairs={{0,1},{1,0},{2,3},{3,2},{4,5},{5,4},{6,7},{7,6},{8,9},{9,8},{10,11... | collective-permute-start | bytes 786440 | tf_op jit(solution)/shard_map/ppermute | solution.py:328
  118.6 1.9 %copy-start.7 = (f32[128,512]{1,0:T(8,128)}, f32[128,512]{1,0:T(8,128)S(1)}, u32[]{:S(2)}) copy-start(f32[128,512]{1,0:T(8,128)S(1)} %collective-permute-done.7.pair) | copy-start | bytes 786436
  118.6 1.9 %collective-permute-start.8 = (f32[128,512]{1,0:T(8,128)S(1)}, f32[128,512]{1,0:T(8,128)S(1)}, u32[]{:S(2)}, u32[]{:S(2)}) collective-permute-start(f32[128,512]{1,0:T(8,128)S(1)} %collective-permute-done.7.pair), channel_id=1, source_target_pairs={{0,1},{1,0},{2,3},{3,2},{4,5},{5,4},{6,7},{7,6},{8,9},{9,8},{10,11... | collective-permute-start | bytes 786440 | tf_op jit(solution)/shard_map/ppermute | solution.py:328
  120.5 0.7 copy-start.8
  120.5 0.8 copy-start.9
